TPU v7x, 32 devices: a whole 2x2x4 slice. The times are simulated.
32 devices in a mesh: group: 4 (over x, core), tp: 8 (over z, y).
Axes of the slice: x: 2, y: 2, z: 4, core: 2. Of those that a mesh axis runs over, the one named last changes fastest.
Arguments:
- hidden: bfloat16 [512, 8192], P('group', 'tp'), may hold values from -6 to 6
- norm_gain: float32 [2, 8192], P(None, 'tp'), may hold values from 0.25 to 1.75
- anchor: bfloat16 [2, 8192, 8192], P(None, None, 'tp'), may hold values from -0.0625 to 0.0625
- delta_tiles: bfloat16 [32, 2, 64, 4, 128, 128], P('group', None, 'tp'), may hold values from -0.1875 to 0.1875
- tile_rows: int32 [32, 2, 64, 4], P('group', None, 'tp'), may hold values from 0 to 64, as said below
- tenant: int32 [512], P('group'), may hold values from 0 to 31, as said below
Outputs:
- updated: bfloat16 [512, 8192], P('group', 'tp')
Inputs may be any that keep to these rules, and one draw needn't show every extreme that they name: Tenant t is owned by group t // 8; the requests of group g are rows g * 128 to g * 128 + 127. For every other group o, call tenant o * 8 + (g + o) % 8 group g's paired tenant of o. Its tiles lie only on group o unless a program moves them. Of one group's requests at most 32 have tenants of any one other group, and in every draw some group has exactly 32 requests of one other group's tenants, none of them its paired tenant of that group. `tile_rows`: each list of one tenant, layer and column block names 1 to 4 distinct row blocks in its first slots and 64 in the others, which marks an empty slot; some list of every draw has empty slots.
All inputs are finite; a program needn't handle non-finite values.
Results may differ from a plain program's by a relative error of at most 0.0052.
Values may be sent and summed in bfloat16 or wider, within the bound.
No kernel may reach another device: no remote copies, remote signals or barrier semaphores. Data moves between devices by JAX's collectives and lax.ppermute only.
A program may use at most 256 MiB of HBM per device.

v0:
```python
import functools

import jax
import jax.numpy as jnp
from jax import lax
from jax.experimental import pallas as pl
from jax.experimental.pallas import tpu as pltpu
from jax.sharding import PartitionSpec as P


F32 = jnp.float32
BF16 = jnp.bfloat16
EPS = 1e-05


def swap(value, axis, offset):
    size = lax.axis_size(axis)
    return lax.ppermute(value, axis, [(i, i ^ offset) for i in range(size)])


def params(mib, **kw):
    return pltpu.CompilerParams(vmem_limit_bytes=mib * 1024 * 1024, **kw)


def whole():
    return pl.BlockSpec(memory_space=pltpu.VMEM)


def in_place():
    return pl.BlockSpec(memory_space=pl.ANY)


def pick_kernel(n_dest, n_shards, *refs):
    sel_ref = refs[0]
    shard_refs = refs[1 : 1 + n_shards]
    out_refs = refs[1 + n_shards :]
    cap = out_refs[0].shape[0]
    width = shard_refs[0].shape[1]
    for s, shard in enumerate(shard_refs):
        rows = jnp.dot(sel_ref[...], shard[...], preferred_element_type=F32).astype(BF16)
        for d in range(n_dest):
            out_refs[d][:, s * width : (s + 1) * width] = rows[d * cap : (d + 1) * cap]


def pick_rows(sel, shards, cap):
    n_dest = sel.shape[0] // cap
    width = shards[0].shape[1] * len(shards)
    nbytes = sum(x.size for x in shards) * 2 + n_dest * cap * width * 2
    return pl.pallas_call(
        functools.partial(pick_kernel, n_dest, len(shards)),
        out_shape=[jax.ShapeDtypeStruct((cap, width), BF16)] * n_dest,
        in_specs=[whole()] * (1 + len(shards)),
        out_specs=[whole()] * n_dest,
        compiler_params=params(8),
        cost_estimate=pl.CostEstimate(
            flops=2 * sel.size * width, bytes_accessed=nbytes, transcendentals=0
        ),
        name="pick_rows",
    )(sel, *shards)


def product_kernel(cfg, ids_ref, *refs):
    n_in, plan, with_anchor, n_slots, per_list, col_step, width = cfg
    src = refs[:n_in]
    slot_ref, tiles_ref = refs[n_in], refs[n_in + 1]
    at = n_in + 2
    if with_anchor:
        anchor_ref, stream_ref, inverse_ref = refs[at : at + 3]
        out_ref, scale_ref = refs[at + 3 : at + 5]
        at += 5
    else:
        out_ref = refs[at]
        at += 1
    full, masks, sem = refs[at : at + 3]
    rows = full.shape[1]
    shards = full.shape[0] - 1
    group = n_slots * per_list
    tile = masks.shape[2]
    step = pl.program_id(0)
    per_shard = width // tile
    shift = per_shard.bit_length() - 1

    def copies():
        out = []
        for i, places in enumerate(plan):
            for at_col, shard, at_row, n_rows in places:
                out.append(
                    pltpu.make_async_copy(
                        src[i].at[:, pl.ds(at_col, width)],
                        full.at[shard, pl.ds(at_row, n_rows)],
                        sem.at[len(out)],
                    )
                )
        return out

    @pl.when(step == 0)
    def _():
        for copy in copies():
            copy.start()
        slots = slot_ref[...]
        for t in range(n_slots):
            masks[t] = jnp.where(slots == t, 1.0, 0.0).astype(BF16)
        full[shards, :, 0:tile] = jnp.zeros((rows, tile), BF16)
        for copy in copies():
            copy.wait()
        if with_anchor:
            squares = jnp.zeros((rows, tile), F32)
            for p in range(shards):
                for k in range(per_shard):
                    lanes = slice(k * tile, (k + 1) * tile)
                    value = full[p, :, lanes].astype(F32) * inverse_ref[p : p + 1, lanes]
                    squares += value * value
            mean = jnp.sum(squares, axis=1, keepdims=True) / (width * shards)
            scale_ref[...] = jnp.broadcast_to(lax.rsqrt(mean + EPS), (rows, tile))

    if with_anchor:
        base = ids_ref[0]
        anchor_out = jnp.zeros((rows, col_step * tile), F32)
        for p in range(shards):
            at_row = pl.multiple_of(jnp.bitwise_xor(base, p) * width, width)
            anchor_out += jnp.dot(
                full[p], anchor_ref[0, pl.ds(at_row, width), :], preferred_element_type=F32
            )
        scale = scale_ref[...]

    for c in range(col_step):
        delta = jnp.zeros((rows, tile), F32)
        for t in range(n_slots):
            parts = []
            for s in range(per_list):
                block = ids_ref[1 + (step * col_step + c) * group + t * per_list + s]
                shard = lax.shift_right_logical(block, shift)
                lane = pl.multiple_of(jnp.bitwise_and(block, per_shard - 1) * tile, tile)
                piece = full[shard, :, pl.ds(lane, tile)] * masks[t]
                parts.append(piece)
            delta += jnp.dot(jnp.concatenate(parts, axis=1), tiles_ref[t, 0, c].reshape(per_list * tile, tile), preferred_element_type=F32)
        cols = slice(c * tile, (c + 1) * tile)
        if with_anchor:
            own = (delta * scale).astype(BF16).astype(F32)
            out_ref[:, cols] = stream_ref[:, cols] + anchor_out[:, cols] * scale + own
        else:
            out_ref[:, cols] = delta.astype(BF16)


def products(ids, sources, plan, rows, slots, tiles, layer, col_step, extra=None):
    n_slots, _, n_cols, per_list, tile, _ = tiles.shape
    shards = 1 + max(place[1] for places in plan for place in places)
    width = n_cols * tile
    with_anchor = extra is not None
    cfg = (len(sources), plan, with_anchor, n_slots, per_list, col_step, width)
    in_specs = [in_place()] * len(sources)
    in_specs += [
        whole(),
        pl.BlockSpec(
            (n_slots, 1, col_step, per_list, tile, tile), lambda i, ids: (0, layer, i, 0, 0, 0)
        ),
    ]
    operands = [*sources, slots, tiles]
    out_shape = jax.ShapeDtypeStruct((rows, width), F32 if with_anchor else BF16)
    out_specs = pl.BlockSpec((rows, col_step * tile), lambda i, ids: (0, i))
    nbytes = rows * shards * width * 2 + n_slots * n_cols * per_list * tile * tile * 2
    flops = 2 * rows * width * n_slots * per_list * tile
    if with_anchor:
        in_specs += [
            pl.BlockSpec((1, shards * width, col_step * tile), lambda i, ids: (layer, 0, i)),
            pl.BlockSpec((rows, col_step * tile), lambda i, ids: (0, i)),
            whole(),
        ]
        operands += list(extra)
        out_shape = [out_shape, jax.ShapeDtypeStruct((rows, tile), F32)]
        out_specs = [out_specs, pl.BlockSpec((rows, tile), lambda i, ids: (0, 0))]
        nbytes += shards * width * width * 2
        flops += 2 * rows * width * shards * width
    n_copies = sum(len(places) for places in plan)
    return pl.pallas_call(
        functools.partial(product_kernel, cfg),
        out_shape=out_shape,
        grid_spec=pltpu.PrefetchScalarGridSpec(
            num_scalar_prefetch=1,
            grid=(n_cols // col_step,),
            in_specs=in_specs,
            out_specs=out_specs,
            scratch_shapes=[
                pltpu.VMEM((shards + 1, rows, width), BF16),
                pltpu.VMEM((n_slots, rows, tile), BF16),
                pltpu.SemaphoreType.DMA((n_copies,)),
            ],
        ),
        compiler_params=params(44, dimension_semantics=("arbitrary",)),
        cost_estimate=pl.CostEstimate(flops=flops, bytes_accessed=nbytes, transcendentals=0),
        name="own_products" if with_anchor else "sent_products",
    )(ids, *operands)


def join_kernel(n_dest, last, *refs):
    partial_ref, back_ref, scale_ref = refs[:3]
    rets = refs[3 : 3 + n_dest]
    cap = rets[0].shape[0]
    tile = scale_ref.shape[1]
    delta = jnp.zeros(partial_ref.shape, F32)
    for d in range(n_dest):
        delta += jnp.dot(
            back_ref[:, d * cap : (d + 1) * cap], rets[d][...], preferred_element_type=F32
        )
    scale = scale_ref[...]
    for k in range(partial_ref.shape[1] // tile):
        cols = slice(k * tile, (k + 1) * tile)
        routed = (delta[:, cols] * scale).astype(BF16).astype(F32)
        stream = partial_ref[:, cols] + routed
        if last:
            refs[3 + n_dest][:, cols] = stream.astype(BF16)
        else:
            gain_ref, stream_ref, y_ref = refs[3 + n_dest :]
            stream_ref[:, cols] = stream
            y_ref[:, cols] = (stream * gain_ref[:, cols]).astype(BF16)


def join(partial, back, scale, rets, gain):
    rows, width = partial.shape
    last = gain is None
    if last:
        out_shape = jax.ShapeDtypeStruct((rows, width), BF16)
        extra = []
    else:
        out_shape = [
            jax.ShapeDtypeStruct((rows, width), F32),
            jax.ShapeDtypeStruct((rows, width), BF16),
        ]
        extra = [gain]
    return pl.pallas_call(
        functools.partial(join_kernel, len(rets), last),
        out_shape=out_shape,
        in_specs=[whole()] * (3 + len(rets) + len(extra)),
        out_specs=whole() if last else [whole()] * 2,
        compiler_params=params(8),
        cost_estimate=pl.CostEstimate(
            flops=4 * rows * width, bytes_accessed=16 * rows * width, transcendentals=0
        ),
        name="join",
    )(partial, back, scale, *rets, *extra)


def gather_gains(norm_gain, pairwise):
    n_layers, width = norm_gain.shape
    count = lax.axis_size("tp")
    if not pairwise:
        gains = lax.all_gather(norm_gain, "tp", axis=1, tiled=True)
        return gains.reshape(n_layers, count, width)
    gains = norm_gain[:, None, :]
    step = 1
    while step < count:
        gains = jnp.concatenate([gains, swap(gains, "tp", step)], axis=1)
        step *= 2
    return gains


def body(hidden, norm_gain, anchor, delta_tiles, tile_rows, tenant):
    groups = lax.axis_size("group")
    tp_count = lax.axis_size("tp")
    my_group = lax.axis_index("group")
    my_tp = lax.axis_index("tp")
    rows, width = hidden.shape
    per_group, n_layers, _, _, tile, _ = delta_tiles.shape
    row_blocks = width * tp_count // tile
    per_shard = width // tile
    cap = rows // 4
    n_dest = groups - 1
    offsets = list(range(1, groups))
    pairwise = tp_count == 8

    stream = hidden.astype(F32)
    y = (stream * norm_gain[0][None, :]).astype(BF16)

    owner = tenant // per_group
    local = tenant % per_group
    dests = jnp.bitwise_xor(my_group, jnp.arange(1, groups, dtype=jnp.int32))
    to_dest = (owner[None, :] == dests[:, None]).astype(jnp.int32)
    rank = jnp.cumsum(to_dest, axis=1) - to_dest
    slot_of = jnp.arange(cap, dtype=jnp.int32)
    hot = (rank[:, None, :] == slot_of[None, :, None]) & (to_dest[:, None, :] > 0)
    hot = hot.reshape(n_dest * cap, rows)
    sel = hot.astype(BF16)
    back = hot.T.astype(BF16)
    labels = jnp.sum(jnp.where(hot, local[None, :] + 1, 0), axis=1).reshape(n_dest, 1, cap)
    got_labels = [swap(labels[i], "group", d) for i, d in enumerate(offsets)]
    got_slots = jnp.concatenate(got_labels, axis=1).reshape(n_dest * cap, 1) - 1
    got_slots = jnp.broadcast_to(got_slots, (n_dest * cap, tile))
    own_slots = jnp.broadcast_to(
        jnp.where(owner == my_group, local, -1)[:, None], (rows, tile)
    )

    base = my_tp if pairwise else jnp.zeros((), jnp.int32)
    blocks = jnp.bitwise_xor(tile_rows, base * per_shard)
    blocks = jnp.where(tile_rows < row_blocks, blocks, row_blocks)
    blocks = blocks.transpose(1, 2, 0, 3).reshape(n_layers, -1)
    ids_of = jnp.concatenate([jnp.full((n_layers, 1), base, jnp.int32), blocks], axis=1)
    inverse = 1.0 / gather_gains(norm_gain, pairwise)

    if pairwise:
        chunks = CHUNKS
        own_plan = tuple(((0, p, 0, rows),) for p in range(tp_count))
    else:
        chunks = (tuple(range(tp_count)),)
        own_plan = (tuple((p * width, p, 0, rows) for p in range(tp_count)),)
    sent_plan = tuple(
        tuple((k * width, p, i * cap, cap) for k, p in enumerate(chunk))
        for i in range(n_dest)
        for chunk in chunks
    )

    for layer in range(n_layers):
        ids = ids_of[layer]
        if pairwise:
            shards = gather_rows(y)
            parts = [[shards[p] for p in chunk] for chunk in chunks]
        else:
            shards = [lax.all_gather(y, "tp", axis=1, tiled=True)]
            parts = [shards]
        sent = [[None] * len(chunks) for _ in range(n_dest)]
        for q, part in enumerate(parts):
            picked = pick_rows(sel, part, cap)
            for i, d in enumerate(offsets):
                sent[i][q] = swap(picked[i], "group", d)
        partial, scale = products(
            ids, shards, own_plan, rows, own_slots, delta_tiles, layer, 2,
            extra=(anchor, stream, inverse[layer]),
        )
        got = [sent[i][q] for i in range(n_dest) for q in range(len(chunks))]
        answers = products(ids, got, sent_plan, n_dest * cap, got_slots, delta_tiles, layer, 2)
        rets = [swap(answers[i * cap : (i + 1) * cap], "group", d) for i, d in enumerate(offsets)]
        if layer + 1 < n_layers:
            gain = norm_gain[layer + 1][None, :]
            stream, y = join(partial, back, scale, rets, gain)
        else:
            updated = join(partial, back, scale, rets, None)
    return updated


CHUNKS = ((0, 1, 2, 4), (5, 6, 3, 7))


def gather_rows(y):
    near = {0: y}
    near[4] = swap(y, "tp", 4)
    near[2] = swap(y, "tp", 2)
    near[1] = swap(y, "tp", 1)
    near[6] = swap(near[4], "tp", 2)
    near[5] = swap(near[4], "tp", 1)
    near[3] = swap(near[2], "tp", 1)
    near[7] = swap(near[5], "tp", 2)
    return [near[p] for p in range(8)]


def solution(mesh):
    return jax.shard_map(
        body,
        mesh=mesh,
        in_specs=(
            P("group", "tp"),
            P(None, "tp"),
            P(None, None, "tp"),
            P("group", None, "tp", None, None, None),
            P("group", None, "tp", None),
            P("group"),
        ),
        out_specs=P("group", "tp"),
        check_vma=False,
    )
```

profile of v0, /device:TPU:0, one launch (start us, length us, event | category | flops | bytes accessed | tf_op | source)
XLA Modules:
  0.0 160.5 jit_solution(10320150263132558914)
XLA Ops:
  0.0 0.8 fusion.8
  0.8 1.0 multiply_convert_fusion.refs_0_.refs_1_
  1.8 3.1 %collective-permute-start = (bf16[128,1024]{1,0:T(8,128)(2,1)S(1)}, bf16[128,1024]{1,0:T(8,128)(2,1)S(1)}, u32[]{:S(2)}, u32[]{:S(2)}) collective-permute-start(bf16[128,1024]{1,0:T(8,128)(2,1)S(1)} %multiply_convert_fusion.refs_0_.refs_1_), channel_id=1, source_target_pairs={{0,1},{1,0},{2,3},{3,2},{4,5},{5,4},{6,7},{7,6},{8,9},{9,8},{10,11... | collective-permute-start | bytes 786440 | tf_op jit(solution)/shard_map/ppermute | solution.py:18
  4.9 1.6 collective-permute-start.1
  6.4 2.6 %collective-permute-start.3 = (bf16[128,1024]{1,0:T(8,128)(2,1)S(1)}, bf16[128,1024]{1,0:T(8,128)(2,1)S(1)}, u32[]{:S(2)}, u32[]{:S(2)}) collective-permute-start(bf16[128,1024]{1,0:T(8,128)(2,1)S(1)} %multiply_convert_fusion.refs_0_.refs_1_), channel_id=1, source_target_pairs={{0,4},{1,5},{2,6},{3,7},{4,0},{5,1},{6,2},{7,3},{8,12},{9,13},{10,... | collective-permute-start | bytes 786440 | tf_op jit(solution)/shard_map/ppermute | solution.py:18
  9.0 0.7 broadcast_in_dim.22
  10.2 0.7 broadcast_add_fusion
  10.9 1.2 compare_select_fusion
  13.6 6.9 %collective-permute-done.3.refs_4_ = bf16[128,1024]{1,0:T(8,128)(2,1)S(1)} collective-permute-done((bf16[128,1024]{1,0:T(8,128)(2,1)S(1)}, bf16[128,1024]{1,0:T(8,128)(2,1)S(1)}, u32[]{:S(2)}, u32[]{:S(2)}) %collective-permute-start.3) | collective-permute-done | bytes 262176 | tf_op jit(solution)/shard_map/ppermute | solution.py:18
  21.1 1.6 collective-permute-start.17
  23.8 1.1 pick_rows.4
  24.8 1.6 collective-permute-start.2
  26.4 1.6 collective-permute-start.5
  28.4 1.4 select_bitcast_fusion
  29.8 1.0 convert_element_type.28.refs_11_
  30.8 0.9 copy.20
  32.0 0.7 pad_maximum_fusion
  33.4 2.6 %collective-permute-start.9 = (f32[2,4,1024]{2,1,0:T(4,128)S(1)}, f32[2,4,1024]{2,1,0:T(4,128)S(1)}, u32[]{:S(2)}, u32[]{:S(2)}) collective-permute-start(f32[2,4,1024]{2,1,0:T(4,128)S(1)} %pad_maximum_fusion), channel_id=1, source_target_pairs={{0,4},{1,5},{2,6},{3,7},{4,0},{5,1},{6,2},{7,3},{8,12},{9,13},{10,... | collective-permute-start | bytes 98312 | tf_op jit(solution)/shard_map/ppermute | solution.py:18
  36.0 0.7 fusion.5
  36.7 0.7 collective-permute-start.12
  38.0 3.1 %collective-permute-done.6.refs_7_.refs_4_ = bf16[128,1024]{1,0:T(8,128)(2,1)S(1)} collective-permute-done((bf16[128,1024]{1,0:T(8,128)(2,1)S(1)}, bf16[128,1024]{1,0:T(8,128)(2,1)S(1)}, u32[]{:S(2)}, u32[]{:S(2)}) %collective-permute-start.6) | collective-permute-done | bytes 262176 | tf_op jit(solution)/shard_map/ppermute | solution.py:18
  42.2 1.2 collective-permute-start.15
  43.4 0.8 maximum_divide_fusion
  44.2 1.7 %collective-permute-done.12.refs_2_ = bf16[32,4096]{1,0:T(8,128)(2,1)S(1)} collective-permute-done((bf16[32,4096]{1,0:T(8,128)(2,1)S(1)}, bf16[32,4096]{1,0:T(8,128)(2,1)S(1)}, u32[]{:S(2)}, u32[]{:S(2)}) %collective-permute-start.12) | collective-permute-done | bytes 262176 | tf_op jit(solution)/shard_map/ppermute | solution.py:18
  45.9 3.8 %collective-permute-done.14.refs_4_ = bf16[32,4096]{1,0:T(8,128)(2,1)S(1)} collective-permute-done((bf16[32,4096]{1,0:T(8,128)(2,1)S(1)}, bf16[32,4096]{1,0:T(8,128)(2,1)S(1)}, u32[]{:S(2)}, u32[]{:S(2)}) %collective-permute-start.14) | collective-permute-done | bytes 262176 | tf_op jit(solution)/shard_map/ppermute | solution.py:18
  49.7 7.4 %collective-permute-done.13.refs_3_ = bf16[32,4096]{1,0:T(8,128)(2,1)S(1)} collective-permute-done((bf16[32,4096]{1,0:T(8,128)(2,1)S(1)}, bf16[32,4096]{1,0:T(8,128)(2,1)S(1)}, u32[]{:S(2)}, u32[]{:S(2)}) %collective-permute-start.13) | collective-permute-done | bytes 262176 | tf_op jit(solution)/shard_map/ppermute | solution.py:18
  57.1 3.5 %collective-permute-done.15.refs_5_ = bf16[32,4096]{1,0:T(8,128)(2,1)S(1)} collective-permute-done((bf16[32,4096]{1,0:T(8,128)(2,1)S(1)}, bf16[32,4096]{1,0:T(8,128)(2,1)S(1)}, u32[]{:S(2)}, u32[]{:S(2)}) %collective-permute-start.15) | collective-permute-done | bytes 262176 | tf_op jit(solution)/shard_map/ppermute | solution.py:18
  60.7 6.9 %sent_products.2 = bf16[96,1024]{1,0:T(8,128)(2,1)S(1)} custom-call(s32[257]{0:T(512)S(1)} %get-tuple-element.41.ids_ref, bf16[32,4096]{1,0:T(8,128)(2,1)S(1)} %collective-permute-done.10.refs_0_, bf16[32,4096]{1,0:T(8,128)(2,1)S(1)} %collective-permute-done.11.refs_1_, bf16[32,4096]{1,0:T(8,128)(2,1)S(1)} %collective-permute-done.12.refs_2_, ...), custom_call_target="tpu_custom_call" | custom-call | flops 805306368 | bytes 9961472 | tf_op jit(solution)/shard_map/sent_products/pallas_call | solution.py:175
  67.6 1.0 collective-permute-start.19
  69.2 0.8 collective-permute-start.21
  70.0 0.7 broadcast_in_dim.21.refs_8_
  70.7 12.0 %own_products.2 = (f32[128,1024]{1,0:T(8,128)S(1)}, f32[128,128]{1,0:T(8,128)S(1)}) custom-call(s32[257]{0:T(512)S(1)} %get-tuple-element.41.ids_ref, bf16[128,1024]{1,0:T(8,128)(2,1)S(1)} %multiply_convert_fusion.refs_0_.refs_1_, bf16[128,1024]{1,0:T(8,128)(2,1)S(1)} %collective-permute-done.refs_1_.refs_2_, ...), custom_call_target="tpu_custom_call" | custom-call | flops 3221225472 | bytes 27262976 | tf_op jit(solution)/shard_map/own_products/pallas_call | solution.py:175
  83.6 1.6 %collective-permute-start.23 = (bf16[128,1024]{1,0:T(8,128)(2,1)S(1)}, bf16[128,1024]{1,0:T(8,128)(2,1)S(1)}, u32[]{:S(2)}, u32[]{:S(2)}) collective-permute-start(bf16[128,1024]{1,0:T(8,128)(2,1)S(1)} %get-tuple-element.31.refs_0_.refs_1_), channel_id=1, source_target_pairs={{0,2},{1,3},{2,0},{3,1},{4,6},{5,7},{6,4},{7,5},{8,10},{9,11},{10,... | collective-permute-start | bytes 786440 | tf_op jit(solution)/shard_map/ppermute | solution.py:18
  85.2 13.1 %collective-permute-done.25.refs_4_ = bf16[128,1024]{1,0:T(8,128)(2,1)S(1)} collective-permute-done((bf16[128,1024]{1,0:T(8,128)(2,1)S(1)}, bf16[128,1024]{1,0:T(8,128)(2,1)S(1)}, u32[]{:S(2)}, u32[]{:S(2)}) %collective-permute-start.25) | collective-permute-done | bytes 262176 | tf_op jit(solution)/shard_map/ppermute | solution.py:18
  98.8 1.5 collective-permute-start.22
  100.8 6.6 %collective-permute-done.26.refs_5_.refs_1_ = bf16[128,1024]{1,0:T(8,128)(2,1)S(1)} collective-permute-done((bf16[128,1024]{1,0:T(8,128)(2,1)S(1)}, bf16[128,1024]{1,0:T(8,128)(2,1)S(1)}, u32[]{:S(2)}, u32[]{:S(2)}) %collective-permute-start.26) | collective-permute-done | bytes 262176 | tf_op jit(solution)/shard_map/ppermute | solution.py:18
  107.4 5.6 %collective-permute-done.22.refs_1_.refs_2_ = bf16[128,1024]{1,0:T(8,128)(2,1)S(1)} collective-permute-done((bf16[128,1024]{1,0:T(8,128)(2,1)S(1)}, bf16[128,1024]{1,0:T(8,128)(2,1)S(1)}, u32[]{:S(2)}, u32[]{:S(2)}) %collective-permute-start.22) | collective-permute-done | bytes 262176 | tf_op jit(solution)/shard_map/ppermute | solution.py:18
  114.1 3.7 %collective-permute-done.24.refs_3_ = bf16[128,1024]{1,0:T(8,128)(2,1)S(1)} collective-permute-done((bf16[128,1024]{1,0:T(8,128)(2,1)S(1)}, bf16[128,1024]{1,0:T(8,128)(2,1)S(1)}, u32[]{:S(2)}, u32[]{:S(2)}) %collective-permute-start.24) | collective-permute-done | bytes 262176 | tf_op jit(solution)/shard_map/ppermute | solution.py:18
  118.1 0.7 collective-permute-start.30
  118.8 1.5 collective-permute-start.32
  120.4 2.4 %collective-permute-done.31.refs_2_ = bf16[32,4096]{1,0:T(8,128)(2,1)S(1)} collective-permute-done((bf16[32,4096]{1,0:T(8,128)(2,1)S(1)}, bf16[32,4096]{1,0:T(8,128)(2,1)S(1)}, u32[]{:S(2)}, u32[]{:S(2)}) %collective-permute-start.31) | collective-permute-done | bytes 262176 | tf_op jit(solution)/shard_map/ppermute | solution.py:18
  122.7 4.5 %collective-permute-done.33.refs_4_ = bf16[32,4096]{1,0:T(8,128)(2,1)S(1)} collective-permute-done((bf16[32,4096]{1,0:T(8,128)(2,1)S(1)}, bf16[32,4096]{1,0:T(8,128)(2,1)S(1)}, u32[]{:S(2)}, u32[]{:S(2)}) %collective-permute-start.33) | collective-permute-done | bytes 262176 | tf_op jit(solution)/shard_map/ppermute | solution.py:18
  127.3 6.7 %collective-permute-done.32.refs_3_ = bf16[32,4096]{1,0:T(8,128)(2,1)S(1)} collective-permute-done((bf16[32,4096]{1,0:T(8,128)(2,1)S(1)}, bf16[32,4096]{1,0:T(8,128)(2,1)S(1)}, u32[]{:S(2)}, u32[]{:S(2)}) %collective-permute-start.32) | collective-permute-done | bytes 262176 | tf_op jit(solution)/shard_map/ppermute | solution.py:18
  134.0 4.5 %collective-permute-done.34.refs_5_ = bf16[32,4096]{1,0:T(8,128)(2,1)S(1)} collective-permute-done((bf16[32,4096]{1,0:T(8,128)(2,1)S(1)}, bf16[32,4096]{1,0:T(8,128)(2,1)S(1)}, u32[]{:S(2)}, u32[]{:S(2)}) %collective-permute-start.34) | collective-permute-done | bytes 262176 | tf_op jit(solution)/shard_map/ppermute | solution.py:18
  138.5 6.9 %sent_products.3 = bf16[96,1024]{1,0:T(8,128)(2,1)S(1)} custom-call(s32[257]{0:T(512)S(1)} %get-tuple-element.42.ids_ref, bf16[32,4096]{1,0:T(8,128)(2,1)S(1)} %collective-permute-done.29.refs_0_, bf16[32,4096]{1,0:T(8,128)(2,1)S(1)} %collective-permute-done.30.refs_1_, bf16[32,4096]{1,0:T(8,128)(2,1)S(1)} %collective-permute-done.31.refs_2_, ...), custom_call_target="tpu_custom_call" | custom-call | flops 805306368 | bytes 9961472 | tf_op jit(solution)/shard_map/sent_products/pallas_call | solution.py:175
  146.4 1.0 collective-permute-start.37
  147.3 12.0 %own_products.3 = (f32[128,1024]{1,0:T(8,128)S(1)}, f32[128,128]{1,0:T(8,128)S(1)}) custom-call(s32[257]{0:T(512)S(1)} %get-tuple-element.42.ids_ref, bf16[128,1024]{1,0:T(8,128)(2,1)S(1)} %get-tuple-element.31.refs_0_.refs_1_, bf16[128,1024]{1,0:T(8,128)(2,1)S(1)} %collective-permute-done.22.refs_1_.refs_2_, ...), custom_call_target="tpu_custom_call" | custom-call | flops 3221225472 | bytes 27262976 | tf_op jit(solution)/shard_map/own_products/pallas_call | solution.py:175
  159.3 1.1 join.3
  (73 shorter events, 11.6 us)
Async XLA Ops:
  1.8 21.5 %collective-permute-start = (bf16[128,1024]{1,0:T(8,128)(2,1)S(1)}, bf16[128,1024]{1,0:T(8,128)(2,1)S(1)}, u32[]{:S(2)}, u32[]{:S(2)}) collective-permute-start(bf16[128,1024]{1,0:T(8,128)(2,1)S(1)} %multiply_convert_fusion.refs_0_.refs_1_), channel_id=1, source_target_pairs={{0,1},{1,0},{2,3},{3,2},{4,5},{5,4},{6,7},{7,6},{8,9},{9,8},{10,11... | collective-permute-start | bytes 786440 | tf_op jit(solution)/shard_map/ppermute | solution.py:18
  4.9 18.9 %collective-permute-start.1 = (bf16[128,1024]{1,0:T(8,128)(2,1)S(1)}, bf16[128,1024]{1,0:T(8,128)(2,1)S(1)}, u32[]{:S(2)}, u32[]{:S(2)}) collective-permute-start(bf16[128,1024]{1,0:T(8,128)(2,1)S(1)} %multiply_convert_fusion.refs_0_.refs_1_), channel_id=1, source_target_pairs={{0,2},{1,3},{2,0},{3,1},{4,6},{5,7},{6,4},{7,5},{8,10},{9,11},{10,... | collective-permute-start | bytes 786440 | tf_op jit(solution)/shard_map/ppermute | solution.py:18
  6.4 14.0 %collective-permute-start.3 = (bf16[128,1024]{1,0:T(8,128)(2,1)S(1)}, bf16[128,1024]{1,0:T(8,128)(2,1)S(1)}, u32[]{:S(2)}, u32[]{:S(2)}) collective-permute-start(bf16[128,1024]{1,0:T(8,128)(2,1)S(1)} %multiply_convert_fusion.refs_0_.refs_1_), channel_id=1, source_target_pairs={{0,4},{1,5},{2,6},{3,7},{4,0},{5,1},{6,2},{7,3},{8,12},{9,13},{10,... | collective-permute-start | bytes 786440 | tf_op jit(solution)/shard_map/ppermute | solution.py:18
  9.7 11.4 %collective-permute-start.7 = (f32[2,1,1024]{2,1,0:T(1,128)S(1)}, f32[2,1,1024]{2,1,0:T(1,128)S(1)}, u32[]{:S(2)}, u32[]{:S(2)}) collective-permute-start(f32[2,1,1024]{2,1,0:T(1,128)S(1)} %broadcast_in_dim.22), channel_id=1, source_target_pairs={{0,1},{1,0},{2,3},{3,2},{4,5},{5,4},{6,7},{7,6},{8,9},{9,8},{10,11... | collective-permute-start | bytes 24584 | tf_op jit(solution)/shard_map/ppermute | solution.py:18
  13.2 11.6 %collective-permute-start.18 = (s32[1,32]{1,0:T(1,128)S(1)}, s32[1,32]{1,0:T(1,128)S(1)}, u32[]{:S(2)}, u32[]{:S(2)}) collective-permute-start(s32[1,32]{1,0:T(1,128)S(1)} %get-tuple-element.58), channel_id=1, source_target_pairs={{0,24},{8,16},{16,8},{24,0},{1,25},{9,17},{17,9},{25,1},{2,26},{10... | collective-permute-start | bytes 392 | tf_op jit(solution)/shard_map/ppermute | solution.py:18
  20.5 7.5 %collective-permute-start.4 = (bf16[128,1024]{1,0:T(8,128)(2,1)S(1)}, bf16[128,1024]{1,0:T(8,128)(2,1)S(1)}, u32[]{:S(2)}, u32[]{:S(2)}) collective-permute-start(bf16[128,1024]{1,0:T(8,128)(2,1)S(1)} %collective-permute-done.3.refs_4_), channel_id=1, source_target_pairs={{0,1},{1,0},{2,3},{3,2},{4,5},{5,4},{6,7},{7,6},{8,9},{9,8},{10,11... | collective-permute-start | bytes 786440 | tf_op jit(solution)/shard_map/ppermute | solution.py:18
  21.1 5.3 %collective-permute-start.17 = (s32[1,32]{1,0:T(1,128)S(1)}, s32[1,32]{1,0:T(1,128)}, u32[]{:S(2)}, u32[]{:S(2)}) collective-permute-start(s32[1,32]{1,0:T(1,128)S(1)} %get-tuple-element.59), channel_id=1, source_target_pairs={{0,16},{8,24},{16,0},{24,8},{1,17},{9,25},{17,1},{25,9},{2,18},{10... | collective-permute-start | bytes 392 | tf_op jit(solution)/shard_map/ppermute | solution.py:18
  23.3 8.6 %collective-permute-start.8 = (f32[2,2,1024]{2,1,0:T(2,128)}, f32[2,2,1024]{2,1,0:T(2,128)}, u32[]{:S(2)}, u32[]{:S(2)}) collective-permute-start(f32[2,2,1024]{2,1,0:T(2,128)} %pad_maximum_fusion.1), channel_id=1, source_target_pairs={{0,2},{1,3},{2,0},{3,1},{4,6},{5,7},{6,4},{7,5},{8,10},{9,11},{10,... | collective-permute-start | bytes 49160 | tf_op jit(solution)/shard_map/ppermute | solution.py:18
  24.8 17.4 %collective-permute-start.10 = (bf16[32,4096]{1,0:T(8,128)(2,1)}, bf16[32,4096]{1,0:T(8,128)(2,1)S(1)}, u32[]{:S(2)}, u32[]{:S(2)}) collective-permute-start(bf16[32,4096]{1,0:T(8,128)(2,1)} %get-tuple-element.25), channel_id=1, source_target_pairs={{0,8},{8,0},{16,24},{24,16},{1,9},{9,1},{17,25},{25,17},{2,10},{10... | collective-permute-start | bytes 786440 | tf_op jit(solution)/shard_map/ppermute | solution.py:18
  24.8 1.6 copy-start
  24.8 11.9 %collective-permute-start.2 = (bf16[128,1024]{1,0:T(8,128)(2,1)S(1)}, bf16[128,1024]{1,0:T(8,128)(2,1)S(1)}, u32[]{:S(2)}, u32[]{:S(2)}) collective-permute-start(bf16[128,1024]{1,0:T(8,128)(2,1)S(1)} %collective-permute-done.1.refs_2_.refs_3_), channel_id=1, source_target_pairs={{0,1},{1,0},{2,3},{3,2},{4,5},{5,4},{6,7},{7,6},{8,9},{9,8},{10,11... | collective-permute-start | bytes 786440 | tf_op jit(solution)/shard_map/ppermute | solution.py:18
  26.4 11.0 %collective-permute-start.5 = (bf16[128,1024]{1,0:T(8,128)(2,1)S(1)}, bf16[128,1024]{1,0:T(8,128)(2,1)S(1)}, u32[]{:S(2)}, u32[]{:S(2)}) collective-permute-start(bf16[128,1024]{1,0:T(8,128)(2,1)S(1)} %collective-permute-done.3.refs_4_), channel_id=1, source_target_pairs={{0,2},{1,3},{2,0},{3,1},{4,6},{5,7},{6,4},{7,5},{8,10},{9,11},{10,... | collective-permute-start | bytes 786440 | tf_op jit(solution)/shard_map/ppermute | solution.py:18
  28.0 13.1 %collective-permute-start.6 = (bf16[128,1024]{1,0:T(8,128)(2,1)S(1)}, bf16[128,1024]{1,0:T(8,128)(2,1)S(1)}, u32[]{:S(2)}, u32[]{:S(2)}) collective-permute-start(bf16[128,1024]{1,0:T(8,128)(2,1)S(1)} %collective-permute-done.4.refs_5_.refs_1_), channel_id=1, source_target_pairs={{0,2},{1,3},{2,0},{3,1},{4,6},{5,7},{6,4},{7,5},{8,10},{9,11},{10,... | collective-permute-start | bytes 786440 | tf_op jit(solution)/shard_map/ppermute | solution.py:18
  31.9 1.4 collective-permute-start.16
  33.4 8.2 %collective-permute-start.9 = (f32[2,4,1024]{2,1,0:T(4,128)S(1)}, f32[2,4,1024]{2,1,0:T(4,128)S(1)}, u32[]{:S(2)}, u32[]{:S(2)}) collective-permute-start(f32[2,4,1024]{2,1,0:T(4,128)S(1)} %pad_maximum_fusion), channel_id=1, source_target_pairs={{0,4},{1,5},{2,6},{3,7},{4,0},{5,1},{6,2},{7,3},{8,12},{9,13},{10,... | collective-permute-start | bytes 98312 | tf_op jit(solution)/shard_map/ppermute | solution.py:18
  36.7 9.2 %collective-permute-start.12 = (bf16[32,4096]{1,0:T(8,128)(2,1)S(1)}, bf16[32,4096]{1,0:T(8,128)(2,1)S(1)}, u32[]{:S(2)}, u32[]{:S(2)}) collective-permute-start(bf16[32,4096]{1,0:T(8,128)(2,1)S(1)} %get-tuple-element.27), channel_id=1, source_target_pairs={{0,16},{8,24},{16,0},{24,8},{1,17},{9,25},{17,1},{25,9},{2,18},{10... | collective-permute-start | bytes 786440 | tf_op jit(solution)/shard_map/ppermute | solution.py:18
  37.4 12.3 %collective-permute-start.14 = (bf16[32,4096]{1,0:T(8,128)(2,1)S(1)}, bf16[32,4096]{1,0:T(8,128)(2,1)S(1)}, u32[]{:S(2)}, u32[]{:S(2)}) collective-permute-start(bf16[32,4096]{1,0:T(8,128)(2,1)S(1)} %get-tuple-element.29), channel_id=1, source_target_pairs={{0,24},{8,16},{16,8},{24,0},{1,25},{9,17},{17,9},{25,1},{2,26},{10... | collective-permute-start | bytes 786440 | tf_op jit(solution)/shard_map/ppermute | solution.py:18
  41.5 8.3 %collective-permute-start.11 = (bf16[32,4096]{1,0:T(8,128)(2,1)S(1)}, bf16[32,4096]{1,0:T(8,128)(2,1)S(1)}, u32[]{:S(2)}, u32[]{:S(2)}) collective-permute-start(bf16[32,4096]{1,0:T(8,128)(2,1)S(1)} %get-tuple-element.26), channel_id=1, source_target_pairs={{0,8},{8,0},{16,24},{24,16},{1,9},{9,1},{17,25},{25,17},{2,10},{10... | collective-permute-start | bytes 786440 | tf_op jit(solution)/shard_map/ppermute | solution.py:18
  41.6 15.6 %collective-permute-start.13 = (bf16[32,4096]{1,0:T(8,128)(2,1)S(1)}, bf16[32,4096]{1,0:T(8,128)(2,1)S(1)}, u32[]{:S(2)}, u32[]{:S(2)}) collective-permute-start(bf16[32,4096]{1,0:T(8,128)(2,1)S(1)} %get-tuple-element.28), channel_id=1, source_target_pairs={{0,16},{8,24},{16,0},{24,8},{1,17},{9,25},{17,1},{25,9},{2,18},{10... | collective-permute-start | bytes 786440 | tf_op jit(solution)/shard_map/ppermute | solution.py:18
  42.2 18.4 %collective-permute-start.15 = (bf16[32,4096]{1,0:T(8,128)(2,1)S(1)}, bf16[32,4096]{1,0:T(8,128)(2,1)S(1)}, u32[]{:S(2)}, u32[]{:S(2)}) collective-permute-start(bf16[32,4096]{1,0:T(8,128)(2,1)S(1)} %get-tuple-element.30), channel_id=1, source_target_pairs={{0,24},{8,16},{16,8},{24,0},{1,25},{9,17},{17,9},{25,1},{2,26},{10... | collective-permute-start | bytes 786440 | tf_op jit(solution)/shard_map/ppermute | solution.py:18
  67.6 15.1 %collective-permute-start.19 = (bf16[32,1024]{1,0:T(8,128)(2,1)S(1)}, bf16[32,1024]{1,0:T(8,128)(2,1)S(1)}, u32[]{:S(2)}, u32[]{:S(2)}) collective-permute-start(bf16[32,1024]{1,0:T(8,128)(2,1)S(1)} %get-tuple-element.52), channel_id=1, source_target_pairs={{0,8},{8,0},{16,24},{24,16},{1,9},{9,1},{17,25},{25,17},{2,10},{10... | collective-permute-start | bytes 196616 | tf_op jit(solution)/shard_map/ppermute | solution.py:18
  68.6 14.2 %collective-permute-start.20 = (bf16[32,1024]{1,0:T(8,128)(2,1)S(1)}, bf16[32,1024]{1,0:T(8,128)(2,1)S(1)}, u32[]{:S(2)}, u32[]{:S(2)}) collective-permute-start(bf16[32,1024]{1,0:T(8,128)(2,1)S(1)} %get-tuple-element.51), channel_id=1, source_target_pairs={{0,16},{8,24},{16,0},{24,8},{1,17},{9,25},{17,1},{25,9},{2,18},{10... | collective-permute-start | bytes 196616 | tf_op jit(solution)/shard_map/ppermute | solution.py:18
  69.2 13.5 %collective-permute-start.21 = (bf16[32,1024]{1,0:T(8,128)(2,1)S(1)}, bf16[32,1024]{1,0:T(8,128)(2,1)S(1)}, u32[]{:S(2)}, u32[]{:S(2)}) collective-permute-start(bf16[32,1024]{1,0:T(8,128)(2,1)S(1)} %get-tuple-element.50), channel_id=1, source_target_pairs={{0,24},{8,16},{16,8},{24,0},{1,25},{9,17},{17,9},{25,1},{2,26},{10... | collective-permute-start | bytes 196616 | tf_op jit(solution)/shard_map/ppermute | solution.py:18
  83.2 15.0 %collective-permute-start.25 = (bf16[128,1024]{1,0:T(8,128)(2,1)S(1)}, bf16[128,1024]{1,0:T(8,128)(2,1)S(1)}, u32[]{:S(2)}, u32[]{:S(2)}) collective-permute-start(bf16[128,1024]{1,0:T(8,128)(2,1)S(1)} %get-tuple-element.31.refs_0_.refs_1_), channel_id=1, source_target_pairs={{0,4},{1,5},{2,6},{3,7},{4,0},{5,1},{6,2},{7,3},{8,12},{9,13},{10,... | collective-permute-start | bytes 786440 | tf_op jit(solution)/shard_map/ppermute | solution.py:18
  83.6 16.7 %collective-permute-start.23 = (bf16[128,1024]{1,0:T(8,128)(2,1)S(1)}, bf16[128,1024]{1,0:T(8,128)(2,1)S(1)}, u32[]{:S(2)}, u32[]{:S(2)}) collective-permute-start(bf16[128,1024]{1,0:T(8,128)(2,1)S(1)} %get-tuple-element.31.refs_0_.refs_1_), channel_id=1, source_target_pairs={{0,2},{1,3},{2,0},{3,1},{4,6},{5,7},{6,4},{7,5},{8,10},{9,11},{10,... | collective-permute-start | bytes 786440 | tf_op jit(solution)/shard_map/ppermute | solution.py:18
  98.2 9.2 %collective-permute-start.26 = (bf16[128,1024]{1,0:T(8,128)(2,1)S(1)}, bf16[128,1024]{1,0:T(8,128)(2,1)S(1)}, u32[]{:S(2)}, u32[]{:S(2)}) collective-permute-start(bf16[128,1024]{1,0:T(8,128)(2,1)S(1)} %collective-permute-done.25.refs_4_), channel_id=1, source_target_pairs={{0,1},{1,0},{2,3},{3,2},{4,5},{5,4},{6,7},{7,6},{8,9},{9,8},{10,11... | collective-permute-start | bytes 786440 | tf_op jit(solution)/shard_map/ppermute | solution.py:18
  98.8 14.3 %collective-permute-start.22 = (bf16[128,1024]{1,0:T(8,128)(2,1)S(1)}, bf16[128,1024]{1,0:T(8,128)(2,1)S(1)}, u32[]{:S(2)}, u32[]{:S(2)}) collective-permute-start(bf16[128,1024]{1,0:T(8,128)(2,1)S(1)} %get-tuple-element.31.refs_0_.refs_1_), channel_id=1, source_target_pairs={{0,1},{1,0},{2,3},{3,2},{4,5},{5,4},{6,7},{7,6},{8,9},{9,8},{10,11... | collective-permute-start | bytes 786440 | tf_op jit(solution)/shard_map/ppermute | solution.py:18
  100.3 17.5 %collective-permute-start.24 = (bf16[128,1024]{1,0:T(8,128)(2,1)S(1)}, bf16[128,1024]{1,0:T(8,128)(2,1)S(1)}, u32[]{:S(2)}, u32[]{:S(2)}) collective-permute-start(bf16[128,1024]{1,0:T(8,128)(2,1)S(1)} %collective-permute-done.23.refs_2_.refs_3_), channel_id=1, source_target_pairs={{0,1},{1,0},{2,3},{3,2},{4,5},{5,4},{6,7},{7,6},{8,9},{9,8},{10,11... | collective-permute-start | bytes 786440 | tf_op jit(solution)/shard_map/ppermute | solution.py:18
  100.8 17.0 %collective-permute-start.27 = (bf16[128,1024]{1,0:T(8,128)(2,1)S(1)}, bf16[128,1024]{1,0:T(8,128)(2,1)S(1)}, u32[]{:S(2)}, u32[]{:S(2)}) collective-permute-start(bf16[128,1024]{1,0:T(8,128)(2,1)S(1)} %collective-permute-done.25.refs_4_), channel_id=1, source_target_pairs={{0,2},{1,3},{2,0},{3,1},{4,6},{5,7},{6,4},{7,5},{8,10},{9,11},{10,... | collective-permute-start | bytes 786440 | tf_op jit(solution)/shard_map/ppermute | solution.py:18
  107.4 10.4 %collective-permute-start.28 = (bf16[128,1024]{1,0:T(8,128)(2,1)S(1)}, bf16[128,1024]{1,0:T(8,128)(2,1)S(1)}, u32[]{:S(2)}, u32[]{:S(2)}) collective-permute-start(bf16[128,1024]{1,0:T(8,128)(2,1)S(1)} %collective-permute-done.26.refs_5_.refs_1_), channel_id=1, source_target_pairs={{0,2},{1,3},{2,0},{3,1},{4,6},{5,7},{6,4},{7,5},{8,10},{9,11},{10,... | collective-permute-start | bytes 786440 | tf_op jit(solution)/shard_map/ppermute | solution.py:18
  113.4 7.0 %collective-permute-start.29 = (bf16[32,4096]{1,0:T(8,128)(2,1)S(1)}, bf16[32,4096]{1,0:T(8,128)(2,1)S(1)}, u32[]{:S(2)}, u32[]{:S(2)}) collective-permute-start(bf16[32,4096]{1,0:T(8,128)(2,1)S(1)} %get-tuple-element.35), channel_id=1, source_target_pairs={{0,8},{8,0},{16,24},{24,16},{1,9},{9,1},{17,25},{25,17},{2,10},{10... | collective-permute-start | bytes 786440 | tf_op jit(solution)/shard_map/ppermute | solution.py:18
  113.5 9.2 %collective-permute-start.31 = (bf16[32,4096]{1,0:T(8,128)(2,1)S(1)}, bf16[32,4096]{1,0:T(8,128)(2,1)S(1)}, u32[]{:S(2)}, u32[]{:S(2)}) collective-permute-start(bf16[32,4096]{1,0:T(8,128)(2,1)S(1)} %get-tuple-element.37), channel_id=1, source_target_pairs={{0,16},{8,24},{16,0},{24,8},{1,17},{9,25},{17,1},{25,9},{2,18},{10... | collective-permute-start | bytes 786440 | tf_op jit(solution)/shard_map/ppermute | solution.py:18
  117.8 9.5 %collective-permute-start.33 = (bf16[32,4096]{1,0:T(8,128)(2,1)S(1)}, bf16[32,4096]{1,0:T(8,128)(2,1)S(1)}, u32[]{:S(2)}, u32[]{:S(2)}) collective-permute-start(bf16[32,4096]{1,0:T(8,128)(2,1)S(1)} %get-tuple-element.39), channel_id=1, source_target_pairs={{0,24},{8,16},{16,8},{24,0},{1,25},{9,17},{17,9},{25,1},{2,26},{10... | collective-permute-start | bytes 786440 | tf_op jit(solution)/shard_map/ppermute | solution.py:18
  118.1 9.1 %collective-permute-start.30 = (bf16[32,4096]{1,0:T(8,128)(2,1)S(1)}, bf16[32,4096]{1,0:T(8,128)(2,1)S(1)}, u32[]{:S(2)}, u32[]{:S(2)}) collective-permute-start(bf16[32,4096]{1,0:T(8,128)(2,1)S(1)} %get-tuple-element.36), channel_id=1, source_target_pairs={{0,8},{8,0},{16,24},{24,16},{1,9},{9,1},{17,25},{25,17},{2,10},{10... | collective-permute-start | bytes 786440 | tf_op jit(solution)/shard_map/ppermute | solution.py:18
  118.8 15.1 %collective-permute-start.32 = (bf16[32,4096]{1,0:T(8,128)(2,1)S(1)}, bf16[32,4096]{1,0:T(8,128)(2,1)S(1)}, u32[]{:S(2)}, u32[]{:S(2)}) collective-permute-start(bf16[32,4096]{1,0:T(8,128)(2,1)S(1)} %get-tuple-element.38), channel_id=1, source_target_pairs={{0,16},{8,24},{16,0},{24,8},{1,17},{9,25},{17,1},{25,9},{2,18},{10... | collective-permute-start | bytes 786440 | tf_op jit(solution)/shard_map/ppermute | solution.py:18
  120.4 18.1 %collective-permute-start.34 = (bf16[32,4096]{1,0:T(8,128)(2,1)S(1)}, bf16[32,4096]{1,0:T(8,128)(2,1)S(1)}, u32[]{:S(2)}, u32[]{:S(2)}) collective-permute-start(bf16[32,4096]{1,0:T(8,128)(2,1)S(1)} %get-tuple-element.40), channel_id=1, source_target_pairs={{0,24},{8,16},{16,8},{24,0},{1,25},{9,17},{17,9},{25,1},{2,26},{10... | collective-permute-start | bytes 786440 | tf_op jit(solution)/shard_map/ppermute | solution.py:18
  145.4 13.9 %collective-permute-start.35 = (bf16[32,1024]{1,0:T(8,128)(2,1)S(1)}, bf16[32,1024]{1,0:T(8,128)(2,1)S(1)}, u32[]{:S(2)}, u32[]{:S(2)}) collective-permute-start(bf16[32,1024]{1,0:T(8,128)(2,1)S(1)} %get-tuple-element.49), channel_id=1, source_target_pairs={{0,8},{8,0},{16,24},{24,16},{1,9},{9,1},{17,25},{25,17},{2,10},{10... | collective-permute-start | bytes 196616 | tf_op jit(solution)/shard_map/ppermute | solution.py:18
  145.8 13.5 %collective-permute-start.36 = (bf16[32,1024]{1,0:T(8,128)(2,1)S(1)}, bf16[32,1024]{1,0:T(8,128)(2,1)S(1)}, u32[]{:S(2)}, u32[]{:S(2)}) collective-permute-start(bf16[32,1024]{1,0:T(8,128)(2,1)S(1)} %get-tuple-element.48), channel_id=1, source_target_pairs={{0,16},{8,24},{16,0},{24,8},{1,17},{9,25},{17,1},{25,9},{2,18},{10... | collective-permute-start | bytes 196616 | tf_op jit(solution)/shard_map/ppermute | solution.py:18
  146.4 13.0 %collective-permute-start.37 = (bf16[32,1024]{1,0:T(8,128)(2,1)S(1)}, bf16[32,1024]{1,0:T(8,128)(2,1)S(1)}, u32[]{:S(2)}, u32[]{:S(2)}) collective-permute-start(bf16[32,1024]{1,0:T(8,128)(2,1)S(1)} %get-tuple-element.47), channel_id=1, source_target_pairs={{0,24},{8,16},{16,8},{24,0},{1,25},{9,17},{17,9},{25,1},{2,26},{10... | collective-permute-start | bytes 196616 | tf_op jit(solution)/shard_map/ppermute | solution.py:18
where the time goes:
time: 161 us; the launch traced here: 160 us
  waiting for transfers between devices  74.2 us (46%)
  Pallas kernels  41.4 us (26%)
  starting transfers between devices  31.4 us (20%)
  other arithmetic  8.74 us (5%)
  local copies, waits for them, and re-layouts  4.35 us (3%)
    ppermute x38, waiting for transfers between devices, swap(): return lax.ppermute(value, axis, [(i, i ^ offset) for i in range(size)])  74.2 us
    pallas_call x4, Pallas kernels, products(): pl.pallas_call(functools.partial(product_kernel, cfg), out_shape=out_shap...  37.7 us
    ppermute x38, starting transfers between devices, swap(): return lax.ppermute(value, axis, [(i, i ^ offset) for i in range(size)])  31.4 us
  transfers between devices with their start and end apart: 38, of which 15 were waited for; matrix products, arithmetic and copies ran while one was open for 7% of the time, Pallas kernels for 16%

commit v1 on v0

v1 whole, which is shorter than its diff:
```python
import functools

import jax
import jax.numpy as jnp
from jax import lax
from jax.experimental import pallas as pl
from jax.experimental.pallas import tpu as pltpu
from jax.sharding import PartitionSpec as P


F32 = jnp.float32
BF16 = jnp.bfloat16
EPS = 1e-05


def swap(value, axis, offset):
    size = lax.axis_size(axis)
    return lax.ppermute(value, axis, [(i, i ^ offset) for i in range(size)])


def params(mib, **kw):
    return pltpu.CompilerParams(vmem_limit_bytes=mib * 1024 * 1024, **kw)


def whole():
    return pl.BlockSpec(memory_space=pltpu.VMEM)


def in_place():
    return pl.BlockSpec(memory_space=pl.ANY)


def pick_kernel(n_dest, n_shards, *refs):
    sel_ref = refs[0]
    shard_refs = refs[1 : 1 + n_shards]
    out_refs = refs[1 + n_shards :]
    cap = out_refs[0].shape[0]
    at = 0
    for shard in shard_refs:
        width = shard.shape[1]
        rows = jnp.dot(sel_ref[...], shard[...], preferred_element_type=F32).astype(BF16)
        for d in range(n_dest):
            out_refs[d][:, at : at + width] = rows[d * cap : (d + 1) * cap]
        at += width


def pick_rows(sel, shards, cap):
    n_dest = sel.shape[0] // cap
    width = sum(x.shape[1] for x in shards)
    nbytes = sum(x.size for x in shards) * 2 + n_dest * cap * width * 2
    return pl.pallas_call(
        functools.partial(pick_kernel, n_dest, len(shards)),
        out_shape=[jax.ShapeDtypeStruct((cap, width), BF16)] * n_dest,
        in_specs=[whole()] * (1 + len(shards)),
        out_specs=[whole()] * n_dest,
        compiler_params=params(8),
        cost_estimate=pl.CostEstimate(
            flops=2 * sel.size * width, bytes_accessed=nbytes, transcendentals=0
        ),
        name="pick_rows",
    )(sel, *shards)


def square_sum(total, x_ref, inverse_ref, p, tile):
    for k in range(inverse_ref.shape[1] // tile):
        lanes = slice(k * tile, (k + 1) * tile)
        value = x_ref[:, lanes].astype(F32) * inverse_ref[p : p + 1, lanes]
        total += value * value
    return total


def early_kernel(part, has_prior, tile, ids_ref, *refs):
    xs = refs[: len(part)]
    anchor_ref = refs[len(part)]
    prior = refs[len(part) + 1 : -1]
    sum_ref = refs[-1]
    step = pl.program_id(0)
    width = anchor_ref.shape[2]
    cols = min(2 * tile, width)
    for k in range(len(part)):

        @pl.when(step == k)
        def _(k=k):
            x = xs[k][...]
            for n in range(0, width, cols):
                lanes = slice(n, n + cols)
                value = jnp.dot(x, anchor_ref[0, :, lanes], preferred_element_type=F32)
                if k > 0:
                    value += sum_ref[:, lanes]
                elif has_prior:
                    value += prior[0][:, lanes]
                sum_ref[:, lanes] = value


def early_products(row_of, part, xs, anchor, prior, layer, tile):
    rows, width = xs[0].shape
    return pl.pallas_call(
        functools.partial(early_kernel, part, bool(prior), tile),
        out_shape=jax.ShapeDtypeStruct((rows, width), F32),
        grid_spec=pltpu.PrefetchScalarGridSpec(
            num_scalar_prefetch=1,
            grid=(len(part),),
            in_specs=[whole()] * len(part)
            + [pl.BlockSpec((1, width, width), lambda i, ids: (layer, ids[i], 0))]
            + [whole()] * len(prior),
            out_specs=pl.BlockSpec((rows, width), lambda i, ids: (0, 0)),
        ),
        compiler_params=params(32, dimension_semantics=("arbitrary",)),
        cost_estimate=pl.CostEstimate(
            flops=2 * rows * width * width * len(part),
            bytes_accessed=2 * width * width * len(part),
            transcendentals=0,
        ),
        name="early_products",
    )(row_of, *xs, anchor, *prior)


def stage_kernel(layer, tiles_ref, out_ref, sem):
    copies = [
        pltpu.make_async_copy(tiles_ref.at[t, layer], out_ref.at[t], sem.at[t])
        for t in range(out_ref.shape[0])
    ]
    for copy in copies:
        copy.start()
    for copy in copies:
        copy.wait()


def stage_tiles(tiles, layer):
    shape = tiles.shape[:1] + tiles.shape[2:]
    return pl.pallas_call(
        functools.partial(stage_kernel, layer),
        out_shape=jax.ShapeDtypeStruct(shape, BF16),
        in_specs=[in_place()],
        out_specs=whole(),
        scratch_shapes=[pltpu.SemaphoreType.DMA((shape[0],))],
        compiler_params=params(40),
        cost_estimate=pl.CostEstimate(
            flops=0, bytes_accessed=tiles.size * 2, transcendentals=0
        ),
        name="stage_tiles",
    )(tiles)


def product_kernel(cfg, ids_ref, *refs):
    n_in, plan, label_plan, parts, has_prior, layer, n_cols, col_step, width = cfg
    src = refs[:n_in]
    tiles_ref = refs[n_in]
    at = n_in + 1
    with_anchor = parts is not None
    if with_anchor:
        anchor_ref, stream_ref, inverse_ref = refs[at : at + 3]
        at += 3
        if has_prior:
            sum_ref = refs[at]
            at += 1
        out_ref, scale_ref = refs[at : at + 2]
        at += 2
    else:
        out_ref = refs[at]
        at += 1
    full, labels, masks, sem = refs[at : at + 4]
    rows = full.shape[1]
    shards = full.shape[0] - 1
    n_slots, _, per_list, tile = tiles_ref.shape[:4]
    group = n_slots * per_list
    per_shard = width // tile
    shift = per_shard.bit_length() - 1

    copies = []
    for i, places in enumerate(plan):
        for at_col, shard, at_row, n_rows in places:
            copies.append(
                pltpu.make_async_copy(
                    src[i].at[:, pl.ds(at_col, width)],
                    full.at[shard, pl.ds(at_row, n_rows)],
                    sem.at[len(copies)],
                )
            )
    for i, at_col, at_row, n_rows in label_plan:
        copies.append(
            pltpu.make_async_copy(
                src[i].at[:, pl.ds(at_col, tile)],
                labels.at[pl.ds(at_row, n_rows)],
                sem.at[len(copies)],
            )
        )
    weights = []
    if with_anchor:
        anchor_buf, anchor_sem = refs[at + 4 : at + 6]
        at_row = 0
        for k, part in enumerate(parts):
            n_rows = len(part) * width
            row = pl.multiple_of(ids_ref[part[0]] * width, width) if len(part) == 1 else 0
            weights.append(
                pltpu.make_async_copy(
                    anchor_ref.at[layer, pl.ds(row, n_rows)],
                    anchor_buf.at[pl.ds(at_row, n_rows)],
                    anchor_sem.at[k],
                )
            )
            at_row += n_rows

    for copy in copies + weights:
        copy.start()
    full[shards, :, 0:tile] = jnp.zeros((rows, tile), BF16)
    for copy in copies:
        copy.wait()
    label = labels[...].astype(F32)
    for t in range(n_slots):
        masks[t] = jnp.where(label == t + 1, 1.0, 0.0).astype(BF16)
    if with_anchor:
        squares = jnp.zeros((rows, tile), F32)
        for p in range(shards):
            squares = square_sum(squares, full.at[p], inverse_ref, p, tile)
        mean = jnp.sum(squares, axis=1, keepdims=True) / (width * shards)
        scale_ref[...] = jnp.broadcast_to(lax.rsqrt(mean + EPS), (rows, tile))
        for copy in weights:
            copy.wait()
        step_cols = col_step * tile
        for n in range(0, width, step_cols):
            lanes = slice(n, n + step_cols)
            anchor_out = jnp.zeros((rows, step_cols), F32)
            for k, p in enumerate([p for part in parts for p in part]):
                anchor_out += jnp.dot(
                    full[p],
                    anchor_buf[k * width : (k + 1) * width, lanes],
                    preferred_element_type=F32,
                )
            if has_prior:
                anchor_out += sum_ref[:, lanes]
            for k in range(0, step_cols, tile):
                out = anchor_out[:, k : k + tile] * scale_ref[...]
                out_ref[:, n + k : n + k + tile] = stream_ref[:, n + k : n + k + tile] + out

    def block_step(step, carry):
        for k in range(col_step):
            c = step * col_step + k
            delta = jnp.zeros((rows, tile), F32)
            for t in range(n_slots):
                pieces = []
                for s in range(per_list):
                    block = ids_ref[shards + c * group + t * per_list + s]
                    shard = lax.shift_right_logical(block, shift)
                    lane = pl.multiple_of(jnp.bitwise_and(block, per_shard - 1) * tile, tile)
                    pieces.append(full[shard, :, pl.ds(lane, tile)] * masks[t])
                delta += jnp.dot(
                    jnp.concatenate(pieces, axis=1),
                    tiles_ref[t, c].reshape(per_list * tile, tile),
                    preferred_element_type=F32,
                )
            cols = pl.ds(pl.multiple_of(c * tile, tile), tile)
            if with_anchor:
                out_ref[:, cols] += (delta * scale_ref[...]).astype(BF16).astype(F32)
            else:
                out_ref[:, cols] = delta.astype(BF16)
        return carry

    lax.fori_loop(0, n_cols // col_step, block_step, 0)


def products(
    ids, sources, plan, label_plan, rows, tiles, layer, col_step,
    parts=None, anchor=None, stream=None, inverse=None, prior=(),
):
    n_slots, n_cols, per_list, tile, _ = tiles.shape
    shards = 1 + max(place[1] for places in plan for place in places)
    width = n_cols * tile
    with_anchor = parts is not None
    cfg = (
        len(sources), plan, label_plan, parts, bool(prior), layer, n_cols, col_step, width,
    )
    in_specs = [in_place()] * len(sources) + [whole()]
    operands = [*sources, tiles]
    out_shape = jax.ShapeDtypeStruct((rows, width), F32 if with_anchor else BF16)
    nbytes = rows * shards * width * 2 + n_slots * n_cols * per_list * tile * tile * 2
    flops = 2 * rows * width * n_slots * per_list * tile
    n_copies = sum(len(places) for places in plan) + len(label_plan)
    scratch = [
        pltpu.VMEM((shards + 1, rows, width), BF16),
        pltpu.VMEM((rows, tile), BF16),
        pltpu.VMEM((n_slots, rows, tile), BF16),
        pltpu.SemaphoreType.DMA((n_copies,)),
    ]
    if with_anchor:
        n_late = sum(len(part) for part in parts)
        in_specs += [in_place()] + [whole()] * (2 + len(prior))
        operands += [anchor, stream, inverse, *prior]
        out_shape = [out_shape, jax.ShapeDtypeStruct((rows, tile), F32)]
        scratch += [
            pltpu.VMEM((n_late * width, width), BF16),
            pltpu.SemaphoreType.DMA((len(parts),)),
        ]
        nbytes += n_late * width * width * 2
        flops += 2 * rows * width * n_late * width
    return pl.pallas_call(
        functools.partial(product_kernel, cfg),
        out_shape=out_shape,
        in_specs=[pl.BlockSpec(memory_space=pltpu.SMEM)] + in_specs,
        out_specs=[whole()] * 2 if with_anchor else whole(),
        scratch_shapes=scratch,
        compiler_params=params(32),
        cost_estimate=pl.CostEstimate(flops=flops, bytes_accessed=nbytes, transcendentals=0),
        name="own_products" if with_anchor else "sent_products",
    )(ids, *operands)


def join_kernel(n_dest, last, *refs):
    partial_ref, back_ref, scale_ref = refs[:3]
    rets = refs[3 : 3 + n_dest]
    cap = rets[0].shape[0]
    tile = scale_ref.shape[1]
    delta = jnp.zeros(partial_ref.shape, F32)
    for d in range(n_dest):
        delta += jnp.dot(
            back_ref[:, d * cap : (d + 1) * cap], rets[d][...], preferred_element_type=F32
        )
    scale = scale_ref[...]
    for k in range(partial_ref.shape[1] // tile):
        cols = slice(k * tile, (k + 1) * tile)
        routed = (delta[:, cols] * scale).astype(BF16).astype(F32)
        stream = partial_ref[:, cols] + routed
        if last:
            refs[3 + n_dest][:, cols] = stream.astype(BF16)
        else:
            gain_ref, stream_ref, y_ref = refs[3 + n_dest :]
            stream_ref[:, cols] = stream
            y_ref[:, cols] = (stream * gain_ref[:, cols]).astype(BF16)


def join(partial, back, scale, rets, gain):
    rows, width = partial.shape
    last = gain is None
    if last:
        out_shape = jax.ShapeDtypeStruct((rows, width), BF16)
        extra = []
    else:
        out_shape = [
            jax.ShapeDtypeStruct((rows, width), F32),
            jax.ShapeDtypeStruct((rows, width), BF16),
        ]
        extra = [gain]
    return pl.pallas_call(
        functools.partial(join_kernel, len(rets), last),
        out_shape=out_shape,
        in_specs=[whole()] * (3 + len(rets) + len(extra)),
        out_specs=whole() if last else [whole()] * 2,
        compiler_params=params(8),
        cost_estimate=pl.CostEstimate(
            flops=4 * rows * width, bytes_accessed=16 * rows * width, transcendentals=0
        ),
        name="join",
    )(partial, back, scale, *rets, *extra)


def gather_gains(norm_gain, pairwise):
    n_layers, width = norm_gain.shape
    count = lax.axis_size("tp")
    if not pairwise:
        gains = lax.all_gather(norm_gain, "tp", axis=1, tiled=True)
        return gains.reshape(n_layers, count, width)
    gains = norm_gain[:, None, :]
    step = 1
    while step < count:
        gains = jnp.concatenate([gains, swap(gains, "tp", step)], axis=1)
        step *= 2
    return gains


def body(hidden, norm_gain, anchor, delta_tiles, tile_rows, tenant):
    groups = lax.axis_size("group")
    tp_count = lax.axis_size("tp")
    my_group = lax.axis_index("group")
    my_tp = lax.axis_index("tp")
    rows, width = hidden.shape
    per_group, n_layers, _, _, tile, _ = delta_tiles.shape
    row_blocks = width * tp_count // tile
    per_shard = width // tile
    cap = rows // 4
    n_dest = groups - 1
    offsets = list(range(1, groups))
    pairwise = tp_count == 8

    stream = hidden.astype(F32)
    y = (stream * norm_gain[0][None, :]).astype(BF16)

    owner = tenant // per_group
    local = tenant % per_group
    dests = jnp.bitwise_xor(my_group, jnp.arange(1, groups, dtype=jnp.int32))
    to_dest = (owner[None, :] == dests[:, None]).astype(jnp.int32)
    rank = jnp.cumsum(to_dest, axis=1) - to_dest
    slot_of = jnp.arange(cap, dtype=jnp.int32)
    hot = (rank[:, None, :] == slot_of[None, :, None]) & (to_dest[:, None, :] > 0)
    hot = hot.reshape(n_dest * cap, rows)
    sel = hot.astype(BF16)
    back = hot.T.astype(BF16)
    label = jnp.broadcast_to((local + 1)[:, None], (rows, tile)).astype(BF16)
    own_label = jnp.where((owner == my_group)[:, None], label, 0.0).astype(BF16)

    base = my_tp if pairwise else jnp.zeros((), jnp.int32)
    blocks = jnp.bitwise_xor(tile_rows, base * per_shard)
    blocks = jnp.where(tile_rows < row_blocks, blocks, row_blocks)
    blocks = blocks.transpose(1, 2, 0, 3).reshape(n_layers, -1)
    shard_of = jnp.bitwise_xor(base, jnp.arange(tp_count, dtype=jnp.int32))
    shard_of = jnp.broadcast_to(shard_of[None, :], (n_layers, tp_count))
    ids_of = jnp.concatenate([shard_of, blocks], axis=1)
    inverse = 1.0 / gather_gains(norm_gain, pairwise)

    if pairwise:
        chunks, early, late = CHUNKS, EARLY, tuple((p,) for p in LATE)
        own_plan = tuple(((0, p, 0, rows),) for p in range(tp_count))
        near_plan = (tuple((p * width, p, 0, cap) for p in range(tp_count)),)
    else:
        chunks = (tuple(range(tp_count)),)
        early, late = (), chunks
        own_plan = (tuple((p * width, p, 0, rows) for p in range(tp_count)),)
        near_plan = (tuple((p * width, p, 0, cap) for p in range(tp_count)),)
    far_plan = tuple(
        tuple((k * width, p, i * cap, cap) for k, p in enumerate(chunk))
        for i in range(1, n_dest)
        for chunk in chunks
    )
    sent_plan = near_plan + far_plan
    n_chunks = len(chunks)
    own_labels = ((len(own_plan), 0, 0, rows),)
    sent_labels = ((0, width * tp_count, 0, cap),) + tuple(
        (1 + (i - 1) * n_chunks, len(chunks[0]) * width, i * cap, cap)
        for i in range(1, n_dest)
    )
    own_plan += ((),)

    for layer in range(n_layers):
        ids = ids_of[layer]
        if pairwise:
            shards = gather_rows(y)
            split = [[shards[p] for p in chunk] for chunk in chunks]
        else:
            shards = [lax.all_gather(y, "tp", axis=1, tiled=True)]
            split = [shards]
        far = [[] for _ in range(n_dest)]
        for q, xs in enumerate(split):
            if q == 0:
                xs = xs + [label]
            picked = pick_rows(sel[cap:], xs, cap)
            for i, d in enumerate(offsets[1:]):
                far[i + 1].append(swap(picked[i], "group", d))
        (picked,) = pick_rows(sel[:cap], shards + [label], cap)
        got = [swap(picked, "group", 1)]
        for pieces in far[1:]:
            got += pieces
        tiles = stage_tiles(delta_tiles, layer)
        prior = ()
        for part in early:
            row_of = jnp.stack([jnp.bitwise_xor(base, p) for p in part])
            prior = early_products(
                row_of, part, [shards[p] for p in part], anchor, prior, layer, tile
            )
            prior = (prior,)
        partial, scale = products(
            ids, shards + [own_label], own_plan, own_labels, rows, tiles,
            layer, 2,
            parts=late, anchor=anchor, stream=stream, inverse=inverse[layer],
            prior=prior,
        )
        answers = products(
            ids, got, sent_plan, sent_labels, n_dest * cap, tiles, layer, 2
        )
        rets = [
            swap(answers[i * cap : (i + 1) * cap], "group", d)
            for i, d in enumerate(offsets)
        ]
        if layer + 1 < n_layers:
            gain = norm_gain[layer + 1][None, :]
            stream, y = join(partial, back, scale, rets, gain)
        else:
            updated = join(partial, back, scale, rets, None)
    return updated


CHUNKS = ((0, 1, 2, 4), (5, 6), (3, 7))
EARLY = ((0, 1), (2, 4), (5, 6))
LATE = (3, 7)


def gather_rows(y):
    near = {0: y}
    near[4] = swap(y, "tp", 4)
    near[2] = swap(y, "tp", 2)
    near[1] = swap(y, "tp", 1)
    near[6] = swap(near[4], "tp", 2)
    near[5] = swap(near[4], "tp", 1)
    near[3] = swap(near[2], "tp", 1)
    near[7] = swap(near[5], "tp", 2)
    return [near[p] for p in range(8)]


def solution(mesh):
    return jax.shard_map(
        body,
        mesh=mesh,
        in_specs=(
            P("group", "tp"),
            P(None, "tp"),
            P(None, None, "tp"),
            P("group", None, "tp", None, None, None),
            P("group", None, "tp", None),
            P("group"),
        ),
        out_specs=P("group", "tp"),
        check_vma=False,
    )
```

time: 161 us -> 163 us (1.012)
  waiting for transfers between devices: 74.2 us -> 60.5 us
  Pallas kernels: 41.4 us -> 54.3 us
  starting transfers between devices: 31.4 us -> 36.1 us
  other arithmetic: 8.74 us -> 5.06 us
    pallas_call x0 -> x8, Pallas kernels: none -> 27.3 us  [the longest x6 20.3 us: early_products(): pl.pallas_call(functools.partial(early_kernel, part, bool(prior), tile),...]
    pallas_call x4, Pallas kernels: 37.7 us -> 22.4 us  [products(): pl.pallas_call(functools.partial(product_kernel, cfg), out_shape=out_shap...]
    ppermute x38 -> x37, waiting for transfers between devices: 74.2 us -> 60.5 us  [swap(): return lax.ppermute(value, axis, [(i, i ^ offset) for i in range(size)])]
    ppermute x38 -> x37, starting transfers between devices: 31.4 us -> 36.1 us  [swap(): return lax.ppermute(value, axis, [(i, i ^ offset) for i in range(size)])]
    unnamed x2 -> x6, local copies, waits for them, and re-layouts: 0.01 us -> 3.29 us
  transfers between devices with their start and end apart: 38 -> 37, of which waited for: 15 -> 12; matrix products, arithmetic and copies ran while one was open for 7% -> 4% of each run, Pallas kernels for 16% -> 27%
where the time goes in v1:
time: 163 us; the launch traced here: 162 us
  waiting for transfers between devices  60.5 us (37%)
  Pallas kernels  54.3 us (33%)
  starting transfers between devices  36.1 us (22%)
  local copies, waits for them, and re-layouts  5.73 us (4%)
  other arithmetic  5.06 us (3%)
    ppermute x37, waiting for transfers between devices, swap(): return lax.ppermute(value, axis, [(i, i ^ offset) for i in range(size)])  60.5 us
    ppermute x37, starting transfers between devices, swap(): return lax.ppermute(value, axis, [(i, i ^ offset) for i in range(size)])  36.1 us
    pallas_call x4, Pallas kernels, products(): pl.pallas_call(functools.partial(product_kernel, cfg), out_shape=out_shap...  22.4 us
    pallas_call x6, Pallas kernels, early_products(): pl.pallas_call(functools.partial(early_kernel, part, bool(prior), tile),...  20.3 us
    pallas_call x2, Pallas kernels, stage_tiles(): pl.pallas_call(functools.partial(stage_kernel, layer), out_shape=jax.Shap...  6.95 us
    unnamed x6, local copies, waits for them, and re-layouts  3.29 us
  transfers between devices with their start and end apart: 37, of which 12 were waited for; matrix products, arithmetic and copies ran while one was open for 4% of the time, Pallas kernels for 27%

profile of v1, /device:TPU:0, one launch (start us, length us, event | category | flops | bytes accessed | tf_op | source)
XLA Modules:
  0.0 162.3 jit_solution(4604894954875095046)
XLA Ops:
  0.0 0.8 fusion.6
  0.8 1.0 multiply_convert_fusion.refs_0_.refs_1_
  1.8 3.1 %collective-permute-start = (bf16[128,1024]{1,0:T(8,128)(2,1)S(1)}, bf16[128,1024]{1,0:T(8,128)(2,1)S(1)}, u32[]{:S(2)}, u32[]{:S(2)}) collective-permute-start(bf16[128,1024]{1,0:T(8,128)(2,1)S(1)} %multiply_convert_fusion.refs_0_.refs_1_), channel_id=1, source_target_pairs={{0,1},{1,0},{2,3},{3,2},{4,5},{5,4},{6,7},{7,6},{8,9},{9,8},{10,11... | collective-permute-start | bytes 786440 | tf_op jit(solution)/shard_map/ppermute | solution.py:18
  4.9 1.6 collective-permute-start.1
  6.4 2.6 %collective-permute-start.3 = (bf16[128,1024]{1,0:T(8,128)(2,1)S(1)}, bf16[128,1024]{1,0:T(8,128)(2,1)S(1)}, u32[]{:S(2)}, u32[]{:S(2)}) collective-permute-start(bf16[128,1024]{1,0:T(8,128)(2,1)S(1)} %multiply_convert_fusion.refs_0_.refs_1_), channel_id=1, source_target_pairs={{0,4},{1,5},{2,6},{3,7},{4,0},{5,1},{6,2},{7,3},{8,12},{9,13},{10,... | collective-permute-start | bytes 786440 | tf_op jit(solution)/shard_map/ppermute | solution.py:18
  12.0 0.8 select_bitcast_fusion
  13.6 6.9 %collective-permute-done.3.refs_1_.refs_4_.refs_5_ = bf16[128,1024]{1,0:T(8,128)(2,1)S(1)} collective-permute-done((bf16[128,1024]{1,0:T(8,128)(2,1)S(1)}, bf16[128,1024]{1,0:T(8,128)(2,1)S(1)}, u32[]{:S(2)}, u32[]{:S(2)}) %collective-permute-start.3) | collective-permute-done | bytes 262176 | tf_op jit(solution)/shard_map/ppermute | solution.py:18
  21.6 1.5 collective-permute-start.2
  23.1 4.8 %collective-permute-done.4.refs_0_.refs_5_.refs_6_.refs_1_ = bf16[128,1024]{1,0:T(8,128)(2,1)S(1)} collective-permute-done((bf16[128,1024]{1,0:T(8,128)(2,1)S(1)}, bf16[128,1024]{1,0:T(8,128)(2,1)S(1)}, u32[]{:S(2)}, u32[]{:S(2)}) %collective-permute-start.4) | collective-permute-done | bytes 262176 | tf_op jit(solution)/shard_map/ppermute | solution.py:18
  27.9 2.2 %collective-permute-start.6 = (bf16[128,1024]{1,0:T(8,128)(2,1)S(1)}, bf16[128,1024]{1,0:T(8,128)(2,1)S(1)}, u32[]{:S(2)}, u32[]{:S(2)}) collective-permute-start(bf16[128,1024]{1,0:T(8,128)(2,1)S(1)} %collective-permute-done.4.refs_0_.refs_5_.refs_6_.refs_1_), channel_id=1, source_target_pairs={{0,2},{1,3},{2,0},{3,1},{4,6},{5,7},{6,4},{7,5},{8,10},{9,11},{10,... | collective-permute-start | bytes 786440 | tf_op jit(solution)/shard_map/ppermute | solution.py:18
  30.4 4.6 %collective-permute-done.8 = f32[2,2,1024]{2,1,0:T(2,128)S(1)} collective-permute-done((f32[2,2,1024]{2,1,0:T(2,128)S(1)}, f32[2,2,1024]{2,1,0:T(2,128)S(1)}, u32[]{:S(2)}, u32[]{:S(2)}) %collective-permute-start.8) | collective-permute-done | bytes 16416 | tf_op jit(solution)/shard_map/ppermute | solution.py:18
  35.0 2.0 %collective-permute-start.9 = (f32[2,4,1024]{2,1,0:T(4,128)S(1)}, f32[2,4,1024]{2,1,0:T(4,128)S(1)}, u32[]{:S(2)}, u32[]{:S(2)}) collective-permute-start(f32[2,4,1024]{2,1,0:T(4,128)S(1)} %pad_maximum_fusion), channel_id=1, source_target_pairs={{0,4},{1,5},{2,6},{3,7},{4,0},{5,1},{6,2},{7,3},{8,12},{9,13},{10,... | collective-permute-start | bytes 98312 | tf_op jit(solution)/shard_map/ppermute | solution.py:18
  37.1 1.2 pick_rows.8
  38.4 1.0 convert_element_type.33.refs_11_
  39.5 3.5 %stage_tiles.2.refs_9_.refs_7_ = bf16[8,8,4,128,128]{4,3,2,1,0:T(8,128)(2,1)S(1)} custom-call(bf16[8,2,8,4,128,128]{5,4,3,2,1,0:T(8,128)(2,1)} %tiles_ref.3), custom_call_target="tpu_custom_call" | custom-call | bytes 16777216 | tf_op jit(solution)/shard_map/stage_tiles/pallas_call | solution.py:131
  43.0 3.3 %copy-done = bf16[8,8,4,128,128]{4,3,2,1,0:T(8,128)(2,1)} copy-done((bf16[8,8,4,128,128]{4,3,2,1,0:T(8,128)(2,1)}, bf16[8,8,4,128,128]{4,3,2,1,0:T(8,128)(2,1)S(1)}, u32[]{:S(2)}) %copy-start) | copy-done | bytes 8388632
  46.7 1.6 collective-permute-start.11
  48.9 1.6 collective-permute-start.12
  50.8 5.3 %collective-permute-done.11.refs_1_ = bf16[32,4224]{1,0:T(8,128)(2,1)S(1)} collective-permute-done((bf16[32,4224]{1,0:T(8,128)(2,1)S(1)}, bf16[32,4224]{1,0:T(8,128)(2,1)S(1)}, u32[]{:S(2)}, u32[]{:S(2)}) %collective-permute-start.11) | collective-permute-done | bytes 270368 | tf_op jit(solution)/shard_map/ppermute | solution.py:18
  56.1 1.5 collective-permute-start.13
  57.6 3.4 %collective-permute-done.14.refs_4_ = bf16[32,4224]{1,0:T(8,128)(2,1)S(1)} collective-permute-done((bf16[32,4224]{1,0:T(8,128)(2,1)S(1)}, bf16[32,4224]{1,0:T(8,128)(2,1)S(1)}, u32[]{:S(2)}, u32[]{:S(2)}) %collective-permute-start.14) | collective-permute-done | bytes 270368 | tf_op jit(solution)/shard_map/ppermute | solution.py:18
  61.0 1.8 %collective-permute-start.16 = (bf16[32,2048]{1,0:T(8,128)(2,1)S(1)}, bf16[32,2048]{1,0:T(8,128)(2,1)S(1)}, u32[]{:S(2)}, u32[]{:S(2)}) collective-permute-start(bf16[32,2048]{1,0:T(8,128)(2,1)S(1)} %get-tuple-element.30), channel_id=1, source_target_pairs={{0,24},{8,16},{16,8},{24,0},{1,25},{9,17},{17,9},{25,1},{2,26},{10... | collective-permute-start | bytes 393224 | tf_op jit(solution)/shard_map/ppermute | solution.py:18
  62.8 3.5 %early_products.6.refs_3_ = f32[128,1024]{1,0:T(8,128)S(1)} custom-call(s32[2]{0:T(128)S(1)} %pad_add_fusion.3.ids_ref, bf16[128,1024]{1,0:T(8,128)(2,1)S(1)} %multiply_convert_fusion.refs_0_.refs_1_, bf16[128,1024]{1,0:T(8,128)(2,1)S(1)} %collective-permute-done.refs_1_.refs_2_, bf16[2,8192,1024]{2,1,0:T(8,128)(2,1)} %refs_10_.3), custom_call_target="tpu_custom_call" | custom-call | flops 536870912 | bytes 4194304 | tf_op jit(solution)/shard_map/early_products/pallas_call | solution.py:97
  66.3 3.5 %early_products.7.refs_3_ = f32[128,1024]{1,0:T(8,128)S(1)} custom-call(s32[2]{0:T(128)S(1)} %pad_add_fusion.2.ids_ref, bf16[128,1024]{1,0:T(8,128)(2,1)S(1)} %collective-permute-done.1.refs_0_.refs_2_.refs_3_, bf16[128,1024]{1,0:T(8,128)(2,1)S(1)} %collective-permute-done.3.refs_1_.refs_4_.refs_5_, bf16[2,8192,1024]{2,1,0:T(8,128)(2,1)} %refs_10_.3, ...), custom_call_target="tpu_custom_call" | custom-call | flops 536870912 | bytes 4194304 | tf_op jit(solution)/shard_map/early_products/pallas_call | solution.py:97
  69.8 3.5 %early_products.8.refs_13_ = f32[128,1024]{1,0:T(8,128)S(1)} custom-call(s32[2]{0:T(128)S(1)} %pad_add_fusion.1.ids_ref, bf16[128,1024]{1,0:T(8,128)(2,1)S(1)} %collective-permute-done.4.refs_0_.refs_5_.refs_6_.refs_1_, bf16[128,1024]{1,0:T(8,128)(2,1)S(1)} %collective-permute-done.5.refs_1_.refs_6_.refs_7_.refs_2_, bf16[2,8192,1024]{2,1,0:T(8,128)(2,1)} %refs_10_.3, ...), custom_call_target="tpu_custom_call" | custom-call | flops 536870912 | bytes 4194304 | tf_op jit(solution)/shard_map/early_products/pallas_call | solution.py:97
  73.5 4.1 %sent_products.2 = bf16[96,1024]{1,0:T(8,128)(2,1)S(1)} custom-call(s32[264]{0:T(512)S(1)} %get-tuple-element.41.ids_ref, bf16[32,8320]{1,0:T(8,128)(2,1)S(1)} %collective-permute-done.10.refs_0_, bf16[32,4224]{1,0:T(8,128)(2,1)S(1)} %collective-permute-done.11.refs_1_, bf16[32,2048]{1,0:T(8,128)(2,1)S(1)} %collective-permute-done.12.refs_2_, ...), custom_call_target="tpu_custom_call" | custom-call | flops 805306368 | bytes 9961472 | tf_op jit(solution)/shard_map/sent_products/pallas_call | solution.py:296
  78.2 1.3 collective-permute-start.19
  79.5 7.1 %own_products.2 = (f32[128,1024]{1,0:T(8,128)S(1)}, f32[128,128]{1,0:T(8,128)S(1)}) custom-call(s32[264]{0:T(512)S(1)} %get-tuple-element.41.ids_ref, bf16[128,1024]{1,0:T(8,128)(2,1)S(1)} %multiply_convert_fusion.refs_0_.refs_1_, bf16[128,1024]{1,0:T(8,128)(2,1)S(1)} %collective-permute-done.refs_1_.refs_2_, ...), custom_call_target="tpu_custom_call" | custom-call | flops 1610612736 | bytes 14680064 | tf_op jit(solution)/shard_map/own_products/pallas_call | solution.py:296
  87.1 1.0 collective-permute-start.23
  88.1 2.1 %collective-permute-start.21 = (bf16[128,1024]{1,0:T(8,128)(2,1)S(1)}, bf16[128,1024]{1,0:T(8,128)(2,1)S(1)}, u32[]{:S(2)}, u32[]{:S(2)}) collective-permute-start(bf16[128,1024]{1,0:T(8,128)(2,1)S(1)} %get-tuple-element.31.refs_0_.refs_1_), channel_id=1, source_target_pairs={{0,2},{1,3},{2,0},{3,1},{4,6},{5,7},{6,4},{7,5},{8,10},{9,11},{10,... | collective-permute-start | bytes 786440 | tf_op jit(solution)/shard_map/ppermute | solution.py:18
  90.2 12.0 %collective-permute-done.23.refs_1_.refs_4_.refs_5_ = bf16[128,1024]{1,0:T(8,128)(2,1)S(1)} collective-permute-done((bf16[128,1024]{1,0:T(8,128)(2,1)S(1)}, bf16[128,1024]{1,0:T(8,128)(2,1)S(1)}, u32[]{:S(2)}, u32[]{:S(2)}) %collective-permute-start.23) | collective-permute-done | bytes 262176 | tf_op jit(solution)/shard_map/ppermute | solution.py:18
  102.8 1.4 collective-permute-start.20
  104.8 6.6 %collective-permute-done.24.refs_0_.refs_5_.refs_6_.refs_1_ = bf16[128,1024]{1,0:T(8,128)(2,1)S(1)} collective-permute-done((bf16[128,1024]{1,0:T(8,128)(2,1)S(1)}, bf16[128,1024]{1,0:T(8,128)(2,1)S(1)}, u32[]{:S(2)}, u32[]{:S(2)}) %collective-permute-start.24) | collective-permute-done | bytes 262176 | tf_op jit(solution)/shard_map/ppermute | solution.py:18
  111.4 5.6 %collective-permute-done.20.refs_1_.refs_2_ = bf16[128,1024]{1,0:T(8,128)(2,1)S(1)} collective-permute-done((bf16[128,1024]{1,0:T(8,128)(2,1)S(1)}, bf16[128,1024]{1,0:T(8,128)(2,1)S(1)}, u32[]{:S(2)}, u32[]{:S(2)}) %collective-permute-start.20) | collective-permute-done | bytes 262176 | tf_op jit(solution)/shard_map/ppermute | solution.py:18
  117.0 4.6 %collective-permute-done.22.refs_3_.refs_4_.refs_1_ = bf16[128,1024]{1,0:T(8,128)(2,1)S(1)} collective-permute-done((bf16[128,1024]{1,0:T(8,128)(2,1)S(1)}, bf16[128,1024]{1,0:T(8,128)(2,1)S(1)}, u32[]{:S(2)}, u32[]{:S(2)}) %collective-permute-start.22) | collective-permute-done | bytes 262176 | tf_op jit(solution)/shard_map/ppermute | solution.py:18
  123.0 1.3 collective-permute-start.31
  124.4 3.5 %stage_tiles.3.refs_9_.refs_7_ = bf16[8,8,4,128,128]{4,3,2,1,0:T(8,128)(2,1)S(1)} custom-call(bf16[8,2,8,4,128,128]{5,4,3,2,1,0:T(8,128)(2,1)} %tiles_ref.3), custom_call_target="tpu_custom_call" | custom-call | bytes 16777216 | tf_op jit(solution)/shard_map/stage_tiles/pallas_call | solution.py:131
  128.7 1.1 collective-permute-start.32
  130.0 1.9 %collective-permute-done.28.refs_1_ = bf16[32,4224]{1,0:T(8,128)(2,1)S(1)} collective-permute-done((bf16[32,4224]{1,0:T(8,128)(2,1)S(1)}, bf16[32,4224]{1,0:T(8,128)(2,1)S(1)}, u32[]{:S(2)}, u32[]{:S(2)}) %collective-permute-start.28) | collective-permute-done | bytes 270368 | tf_op jit(solution)/shard_map/ppermute | solution.py:18
  132.4 4.3 %collective-permute-done.31.refs_4_ = bf16[32,4224]{1,0:T(8,128)(2,1)S(1)} collective-permute-done((bf16[32,4224]{1,0:T(8,128)(2,1)S(1)}, bf16[32,4224]{1,0:T(8,128)(2,1)S(1)}, u32[]{:S(2)}, u32[]{:S(2)}) %collective-permute-start.31) | collective-permute-done | bytes 270368 | tf_op jit(solution)/shard_map/ppermute | solution.py:18
  136.7 0.9 collective-permute-start.33
  137.6 3.2 %early_products.9.refs_3_ = f32[128,1024]{1,0:T(8,128)S(1)} custom-call(s32[2]{0:T(128)S(1)} %pad_add_fusion.3.ids_ref, bf16[128,1024]{1,0:T(8,128)(2,1)S(1)} %get-tuple-element.31.refs_0_.refs_1_, bf16[128,1024]{1,0:T(8,128)(2,1)S(1)} %collective-permute-done.20.refs_1_.refs_2_, bf16[2,8192,1024]{2,1,0:T(8,128)(2,1)} %refs_10_.3), custom_call_target="tpu_custom_call" | custom-call | flops 536870912 | bytes 4194304 | tf_op jit(solution)/shard_map/early_products/pallas_call | solution.py:97
  140.9 3.3 %early_products.10.refs_3_ = f32[128,1024]{1,0:T(8,128)S(1)} custom-call(s32[2]{0:T(128)S(1)} %pad_add_fusion.2.ids_ref, bf16[128,1024]{1,0:T(8,128)(2,1)S(1)} %collective-permute-done.21.refs_0_.refs_2_.refs_3_, bf16[128,1024]{1,0:T(8,128)(2,1)S(1)} %collective-permute-done.23.refs_1_.refs_4_.refs_5_, bf16[2,8192,1024]{2,1,0:T(8,128)(2,1)} %refs_10_.3, ...), custom_call_target="tpu_custom_call" | custom-call | flops 536870912 | bytes 4194304 | tf_op jit(solution)/shard_map/early_products/pallas_call | solution.py:97
  144.2 3.3 %early_products.11.refs_13_ = f32[128,1024]{1,0:T(8,128)S(1)} custom-call(s32[2]{0:T(128)S(1)} %pad_add_fusion.1.ids_ref, bf16[128,1024]{1,0:T(8,128)(2,1)S(1)} %collective-permute-done.24.refs_0_.refs_5_.refs_6_.refs_1_, bf16[128,1024]{1,0:T(8,128)(2,1)S(1)} %collective-permute-done.25.refs_1_.refs_6_.refs_7_.refs_2_, bf16[2,8192,1024]{2,1,0:T(8,128)(2,1)} %refs_10_.3, ...), custom_call_target="tpu_custom_call" | custom-call | flops 536870912 | bytes 4194304 | tf_op jit(solution)/shard_map/early_products/pallas_call | solution.py:97
  148.0 4.0 %sent_products.3 = bf16[96,1024]{1,0:T(8,128)(2,1)S(1)} custom-call(s32[264]{0:T(512)S(1)} %get-tuple-element.42.ids_ref, bf16[32,8320]{1,0:T(8,128)(2,1)S(1)} %collective-permute-done.27.refs_0_, bf16[32,4224]{1,0:T(8,128)(2,1)S(1)} %collective-permute-done.28.refs_1_, bf16[32,2048]{1,0:T(8,128)(2,1)S(1)} %collective-permute-done.29.refs_2_, ...), custom_call_target="tpu_custom_call" | custom-call | flops 805306368 | bytes 9961472 | tf_op jit(solution)/shard_map/sent_products/pallas_call | solution.py:296
  152.4 0.8 collective-permute-start.35
  154.0 7.1 %own_products.3 = (f32[128,1024]{1,0:T(8,128)S(1)}, f32[128,128]{1,0:T(8,128)S(1)}) custom-call(s32[264]{0:T(512)S(1)} %get-tuple-element.42.ids_ref, bf16[128,1024]{1,0:T(8,128)(2,1)S(1)} %get-tuple-element.31.refs_0_.refs_1_, bf16[128,1024]{1,0:T(8,128)(2,1)S(1)} %collective-permute-done.20.refs_1_.refs_2_, ...), custom_call_target="tpu_custom_call" | custom-call | flops 1610612736 | bytes 14680064 | tf_op jit(solution)/shard_map/own_products/pallas_call | solution.py:296
  161.1 1.1 join.3
  (93 shorter events, 13.7 us)
Async XLA Ops:
  1.8 35.2 %collective-permute-start = (bf16[128,1024]{1,0:T(8,128)(2,1)S(1)}, bf16[128,1024]{1,0:T(8,128)(2,1)S(1)}, u32[]{:S(2)}, u32[]{:S(2)}) collective-permute-start(bf16[128,1024]{1,0:T(8,128)(2,1)S(1)} %multiply_convert_fusion.refs_0_.refs_1_), channel_id=1, source_target_pairs={{0,1},{1,0},{2,3},{3,2},{4,5},{5,4},{6,7},{7,6},{8,9},{9,8},{10,11... | collective-permute-start | bytes 786440 | tf_op jit(solution)/shard_map/ppermute | solution.py:18
  4.9 16.8 %collective-permute-start.1 = (bf16[128,1024]{1,0:T(8,128)(2,1)S(1)}, bf16[128,1024]{1,0:T(8,128)(2,1)S(1)}, u32[]{:S(2)}, u32[]{:S(2)}) collective-permute-start(bf16[128,1024]{1,0:T(8,128)(2,1)S(1)} %multiply_convert_fusion.refs_0_.refs_1_), channel_id=1, source_target_pairs={{0,2},{1,3},{2,0},{3,1},{4,6},{5,7},{6,4},{7,5},{8,10},{9,11},{10,... | collective-permute-start | bytes 786440 | tf_op jit(solution)/shard_map/ppermute | solution.py:18
  6.4 14.0 %collective-permute-start.3 = (bf16[128,1024]{1,0:T(8,128)(2,1)S(1)}, bf16[128,1024]{1,0:T(8,128)(2,1)S(1)}, u32[]{:S(2)}, u32[]{:S(2)}) collective-permute-start(bf16[128,1024]{1,0:T(8,128)(2,1)S(1)} %multiply_convert_fusion.refs_0_.refs_1_), channel_id=1, source_target_pairs={{0,4},{1,5},{2,6},{3,7},{4,0},{5,1},{6,2},{7,3},{8,12},{9,13},{10,... | collective-permute-start | bytes 786440 | tf_op jit(solution)/shard_map/ppermute | solution.py:18
  9.7 20.4 %collective-permute-start.7 = (f32[2,1,1024]{2,1,0:T(1,128)S(1)}, f32[2,1,1024]{2,1,0:T(1,128)S(1)}, u32[]{:S(2)}, u32[]{:S(2)}) collective-permute-start(f32[2,1,1024]{2,1,0:T(1,128)S(1)} %broadcast_in_dim.24), channel_id=1, source_target_pairs={{0,1},{1,0},{2,3},{3,2},{4,5},{5,4},{6,7},{7,6},{8,9},{9,8},{10,11... | collective-permute-start | bytes 24584 | tf_op jit(solution)/shard_map/ppermute | solution.py:18
  20.5 7.4 %collective-permute-start.4 = (bf16[128,1024]{1,0:T(8,128)(2,1)S(1)}, bf16[128,1024]{1,0:T(8,128)(2,1)S(1)}, u32[]{:S(2)}, u32[]{:S(2)}) collective-permute-start(bf16[128,1024]{1,0:T(8,128)(2,1)S(1)} %collective-permute-done.3.refs_1_.refs_4_.refs_5_), channel_id=1, source_target_pairs={{0,1},{1,0},{2,3},{3,2},{4,5},{5,4},{6,7},{7,6},{8,9},{9,8},{10,11... | collective-permute-start | bytes 786440 | tf_op jit(solution)/shard_map/ppermute | solution.py:18
  21.2 15.8 %collective-permute-start.5 = (bf16[128,1024]{1,0:T(8,128)(2,1)S(1)}, bf16[128,1024]{1,0:T(8,128)(2,1)S(1)}, u32[]{:S(2)}, u32[]{:S(2)}) collective-permute-start(bf16[128,1024]{1,0:T(8,128)(2,1)S(1)} %collective-permute-done.3.refs_1_.refs_4_.refs_5_), channel_id=1, source_target_pairs={{0,2},{1,3},{2,0},{3,1},{4,6},{5,7},{6,4},{7,5},{8,10},{9,11},{10,... | collective-permute-start | bytes 786440 | tf_op jit(solution)/shard_map/ppermute | solution.py:18
  21.6 15.4 %collective-permute-start.2 = (bf16[128,1024]{1,0:T(8,128)(2,1)S(1)}, bf16[128,1024]{1,0:T(8,128)(2,1)S(1)}, u32[]{:S(2)}, u32[]{:S(2)}) collective-permute-start(bf16[128,1024]{1,0:T(8,128)(2,1)S(1)} %collective-permute-done.1.refs_0_.refs_2_.refs_3_), channel_id=1, source_target_pairs={{0,1},{1,0},{2,3},{3,2},{4,5},{5,4},{6,7},{7,6},{8,9},{9,8},{10,11... | collective-permute-start | bytes 786440 | tf_op jit(solution)/shard_map/ppermute | solution.py:18
  27.9 9.1 %collective-permute-start.6 = (bf16[128,1024]{1,0:T(8,128)(2,1)S(1)}, bf16[128,1024]{1,0:T(8,128)(2,1)S(1)}, u32[]{:S(2)}, u32[]{:S(2)}) collective-permute-start(bf16[128,1024]{1,0:T(8,128)(2,1)S(1)} %collective-permute-done.4.refs_0_.refs_5_.refs_6_.refs_1_), channel_id=1, source_target_pairs={{0,2},{1,3},{2,0},{3,1},{4,6},{5,7},{6,4},{7,5},{8,10},{9,11},{10,... | collective-permute-start | bytes 786440 | tf_op jit(solution)/shard_map/ppermute | solution.py:18
  30.1 4.9 %collective-permute-start.8 = (f32[2,2,1024]{2,1,0:T(2,128)S(1)}, f32[2,2,1024]{2,1,0:T(2,128)S(1)}, u32[]{:S(2)}, u32[]{:S(2)}) collective-permute-start(f32[2,2,1024]{2,1,0:T(2,128)S(1)} %pad_maximum_fusion.1), channel_id=1, source_target_pairs={{0,2},{1,3},{2,0},{3,1},{4,6},{5,7},{6,4},{7,5},{8,10},{9,11},{10,... | collective-permute-start | bytes 49160 | tf_op jit(solution)/shard_map/ppermute | solution.py:18
  35.0 13.6 %collective-permute-start.9 = (f32[2,4,1024]{2,1,0:T(4,128)S(1)}, f32[2,4,1024]{2,1,0:T(4,128)S(1)}, u32[]{:S(2)}, u32[]{:S(2)}) collective-permute-start(f32[2,4,1024]{2,1,0:T(4,128)S(1)} %pad_maximum_fusion), channel_id=1, source_target_pairs={{0,4},{1,5},{2,6},{3,7},{4,0},{5,1},{6,2},{7,3},{8,12},{9,13},{10,... | collective-permute-start | bytes 98312 | tf_op jit(solution)/shard_map/ppermute | solution.py:18
  38.3 35.1 %collective-permute-start.10 = (bf16[32,8320]{1,0:T(8,128)(2,1)}, bf16[32,8320]{1,0:T(8,128)(2,1)S(1)}, u32[]{:S(2)}, u32[]{:S(2)}) collective-permute-start(bf16[32,8320]{1,0:T(8,128)(2,1)} %pick_rows.8), channel_id=1, source_target_pairs={{0,8},{8,0},{16,24},{24,16},{1,9},{9,1},{17,25},{25,17},{2,10},{10... | collective-permute-start | bytes 1597448 | tf_op jit(solution)/shard_map/ppermute | solution.py:18
  43.0 3.3 %copy-start = (bf16[8,8,4,128,128]{4,3,2,1,0:T(8,128)(2,1)}, bf16[8,8,4,128,128]{4,3,2,1,0:T(8,128)(2,1)S(1)}, u32[]{:S(2)}) copy-start(bf16[8,8,4,128,128]{4,3,2,1,0:T(8,128)(2,1)S(1)} %stage_tiles.2.refs_9_.refs_7_) | copy-start | bytes 25165828
  46.7 9.4 %collective-permute-start.11 = (bf16[32,4224]{1,0:T(8,128)(2,1)S(1)}, bf16[32,4224]{1,0:T(8,128)(2,1)S(1)}, u32[]{:S(2)}, u32[]{:S(2)}) collective-permute-start(bf16[32,4224]{1,0:T(8,128)(2,1)S(1)} %get-tuple-element.25), channel_id=1, source_target_pairs={{0,16},{8,24},{16,0},{24,8},{1,17},{9,25},{17,1},{25,9},{2,18},{10... | collective-permute-start | bytes 811016 | tf_op jit(solution)/shard_map/ppermute | solution.py:18
  48.2 12.7 %collective-permute-start.14 = (bf16[32,4224]{1,0:T(8,128)(2,1)S(1)}, bf16[32,4224]{1,0:T(8,128)(2,1)S(1)}, u32[]{:S(2)}, u32[]{:S(2)}) collective-permute-start(bf16[32,4224]{1,0:T(8,128)(2,1)S(1)} %get-tuple-element.28), channel_id=1, source_target_pairs={{0,24},{8,16},{16,8},{24,0},{1,25},{9,17},{17,9},{25,1},{2,26},{10... | collective-permute-start | bytes 811016 | tf_op jit(solution)/shard_map/ppermute | solution.py:18
  48.9 24.5 %collective-permute-start.12 = (bf16[32,2048]{1,0:T(8,128)(2,1)S(1)}, bf16[32,2048]{1,0:T(8,128)(2,1)S(1)}, u32[]{:S(2)}, u32[]{:S(2)}) collective-permute-start(bf16[32,2048]{1,0:T(8,128)(2,1)S(1)} %get-tuple-element.26), channel_id=1, source_target_pairs={{0,16},{8,24},{16,0},{24,8},{1,17},{9,25},{17,1},{25,9},{2,18},{10... | collective-permute-start | bytes 393224 | tf_op jit(solution)/shard_map/ppermute | solution.py:18
  50.4 23.0 %collective-permute-start.15 = (bf16[32,2048]{1,0:T(8,128)(2,1)S(1)}, bf16[32,2048]{1,0:T(8,128)(2,1)S(1)}, u32[]{:S(2)}, u32[]{:S(2)}) collective-permute-start(bf16[32,2048]{1,0:T(8,128)(2,1)S(1)} %get-tuple-element.29), channel_id=1, source_target_pairs={{0,24},{8,16},{16,8},{24,0},{1,25},{9,17},{17,9},{25,1},{2,26},{10... | collective-permute-start | bytes 393224 | tf_op jit(solution)/shard_map/ppermute | solution.py:18
  56.1 17.3 %collective-permute-start.13 = (bf16[32,2048]{1,0:T(8,128)(2,1)S(1)}, bf16[32,2048]{1,0:T(8,128)(2,1)S(1)}, u32[]{:S(2)}, u32[]{:S(2)}) collective-permute-start(bf16[32,2048]{1,0:T(8,128)(2,1)S(1)} %get-tuple-element.27), channel_id=1, source_target_pairs={{0,16},{8,24},{16,0},{24,8},{1,17},{9,25},{17,1},{25,9},{2,18},{10... | collective-permute-start | bytes 393224 | tf_op jit(solution)/shard_map/ppermute | solution.py:18
  61.0 12.5 %collective-permute-start.16 = (bf16[32,2048]{1,0:T(8,128)(2,1)S(1)}, bf16[32,2048]{1,0:T(8,128)(2,1)S(1)}, u32[]{:S(2)}, u32[]{:S(2)}) collective-permute-start(bf16[32,2048]{1,0:T(8,128)(2,1)S(1)} %get-tuple-element.30), channel_id=1, source_target_pairs={{0,24},{8,16},{16,8},{24,0},{1,25},{9,17},{17,9},{25,1},{2,26},{10... | collective-permute-start | bytes 393224 | tf_op jit(solution)/shard_map/ppermute | solution.py:18
  66.3 7.2 %slice-start = ((s8[8388608]{0:T(1024)(128)(4,1)}), s8[4194304]{0:T(1024)(128)(4,1)S(1)}, s32[]{:S(2)}) async-start(s8[8388608]{0:T(1024)(128)(4,1)} %bitcast.19), calls=%async_computation | async-start | bytes 8388608
  69.8 3.6 %slice-start.1 = ((s8[8388608]{0:T(1024)(128)(4,1)}), s8[4194304]{0:T(1024)(128)(4,1)S(1)}, s32[]{:S(2)}) async-start(s8[8388608]{0:T(1024)(128)(4,1)} %bitcast.19), calls=%async_computation.1 | async-start | bytes 8388608
  77.6 9.1 %collective-permute-start.17 = (bf16[32,1024]{1,0:T(8,128)(2,1)S(1)}, bf16[32,1024]{1,0:T(8,128)(2,1)S(1)}, u32[]{:S(2)}, u32[]{:S(2)}) collective-permute-start(bf16[32,1024]{1,0:T(8,128)(2,1)S(1)} %get-tuple-element.50), channel_id=1, source_target_pairs={{0,8},{8,0},{16,24},{24,16},{1,9},{9,1},{17,25},{25,17},{2,10},{10... | collective-permute-start | bytes 196616 | tf_op jit(solution)/shard_map/ppermute | solution.py:18
  77.6 9.0 %collective-permute-start.18 = (bf16[32,1024]{1,0:T(8,128)(2,1)S(1)}, bf16[32,1024]{1,0:T(8,128)(2,1)S(1)}, u32[]{:S(2)}, u32[]{:S(2)}) collective-permute-start(bf16[32,1024]{1,0:T(8,128)(2,1)S(1)} %get-tuple-element.49), channel_id=1, source_target_pairs={{0,16},{8,24},{16,0},{24,8},{1,17},{9,25},{17,1},{25,9},{2,18},{10... | collective-permute-start | bytes 196616 | tf_op jit(solution)/shard_map/ppermute | solution.py:18
  78.2 8.4 %collective-permute-start.19 = (bf16[32,1024]{1,0:T(8,128)(2,1)S(1)}, bf16[32,1024]{1,0:T(8,128)(2,1)S(1)}, u32[]{:S(2)}, u32[]{:S(2)}) collective-permute-start(bf16[32,1024]{1,0:T(8,128)(2,1)S(1)} %get-tuple-element.48), channel_id=1, source_target_pairs={{0,24},{8,16},{16,8},{24,0},{1,25},{9,17},{17,9},{25,1},{2,26},{10... | collective-permute-start | bytes 196616 | tf_op jit(solution)/shard_map/ppermute | solution.py:18
  87.1 15.1 %collective-permute-start.23 = (bf16[128,1024]{1,0:T(8,128)(2,1)S(1)}, bf16[128,1024]{1,0:T(8,128)(2,1)S(1)}, u32[]{:S(2)}, u32[]{:S(2)}) collective-permute-start(bf16[128,1024]{1,0:T(8,128)(2,1)S(1)} %get-tuple-element.31.refs_0_.refs_1_), channel_id=1, source_target_pairs={{0,4},{1,5},{2,6},{3,7},{4,0},{5,1},{6,2},{7,3},{8,12},{9,13},{10,... | collective-permute-start | bytes 786440 | tf_op jit(solution)/shard_map/ppermute | solution.py:18
  88.1 16.1 %collective-permute-start.21 = (bf16[128,1024]{1,0:T(8,128)(2,1)S(1)}, bf16[128,1024]{1,0:T(8,128)(2,1)S(1)}, u32[]{:S(2)}, u32[]{:S(2)}) collective-permute-start(bf16[128,1024]{1,0:T(8,128)(2,1)S(1)} %get-tuple-element.31.refs_0_.refs_1_), channel_id=1, source_target_pairs={{0,2},{1,3},{2,0},{3,1},{4,6},{5,7},{6,4},{7,5},{8,10},{9,11},{10,... | collective-permute-start | bytes 786440 | tf_op jit(solution)/shard_map/ppermute | solution.py:18
  102.2 9.2 %collective-permute-start.24 = (bf16[128,1024]{1,0:T(8,128)(2,1)S(1)}, bf16[128,1024]{1,0:T(8,128)(2,1)S(1)}, u32[]{:S(2)}, u32[]{:S(2)}) collective-permute-start(bf16[128,1024]{1,0:T(8,128)(2,1)S(1)} %collective-permute-done.23.refs_1_.refs_4_.refs_5_), channel_id=1, source_target_pairs={{0,1},{1,0},{2,3},{3,2},{4,5},{5,4},{6,7},{7,6},{8,9},{9,8},{10,11... | collective-permute-start | bytes 786440 | tf_op jit(solution)/shard_map/ppermute | solution.py:18
  102.8 14.2 %collective-permute-start.20 = (bf16[128,1024]{1,0:T(8,128)(2,1)S(1)}, bf16[128,1024]{1,0:T(8,128)(2,1)S(1)}, u32[]{:S(2)}, u32[]{:S(2)}) collective-permute-start(bf16[128,1024]{1,0:T(8,128)(2,1)S(1)} %get-tuple-element.31.refs_0_.refs_1_), channel_id=1, source_target_pairs={{0,1},{1,0},{2,3},{3,2},{4,5},{5,4},{6,7},{7,6},{8,9},{9,8},{10,11... | collective-permute-start | bytes 786440 | tf_op jit(solution)/shard_map/ppermute | solution.py:18
  104.2 17.4 %collective-permute-start.25 = (bf16[128,1024]{1,0:T(8,128)(2,1)S(1)}, bf16[128,1024]{1,0:T(8,128)(2,1)S(1)}, u32[]{:S(2)}, u32[]{:S(2)}) collective-permute-start(bf16[128,1024]{1,0:T(8,128)(2,1)S(1)} %collective-permute-done.23.refs_1_.refs_4_.refs_5_), channel_id=1, source_target_pairs={{0,2},{1,3},{2,0},{3,1},{4,6},{5,7},{6,4},{7,5},{8,10},{9,11},{10,... | collective-permute-start | bytes 786440 | tf_op jit(solution)/shard_map/ppermute | solution.py:18
  104.2 17.4 %collective-permute-start.22 = (bf16[128,1024]{1,0:T(8,128)(2,1)S(1)}, bf16[128,1024]{1,0:T(8,128)(2,1)S(1)}, u32[]{:S(2)}, u32[]{:S(2)}) collective-permute-start(bf16[128,1024]{1,0:T(8,128)(2,1)S(1)} %collective-permute-done.21.refs_0_.refs_2_.refs_3_), channel_id=1, source_target_pairs={{0,1},{1,0},{2,3},{3,2},{4,5},{5,4},{6,7},{7,6},{8,9},{9,8},{10,11... | collective-permute-start | bytes 786440 | tf_op jit(solution)/shard_map/ppermute | solution.py:18
  111.4 10.3 %collective-permute-start.26 = (bf16[128,1024]{1,0:T(8,128)(2,1)S(1)}, bf16[128,1024]{1,0:T(8,128)(2,1)S(1)}, u32[]{:S(2)}, u32[]{:S(2)}) collective-permute-start(bf16[128,1024]{1,0:T(8,128)(2,1)S(1)} %collective-permute-done.24.refs_0_.refs_5_.refs_6_.refs_1_), channel_id=1, source_target_pairs={{0,2},{1,3},{2,0},{3,1},{4,6},{5,7},{6,4},{7,5},{8,10},{9,11},{10,... | collective-permute-start | bytes 786440 | tf_op jit(solution)/shard_map/ppermute | solution.py:18
  122.1 25.9 %collective-permute-start.27 = (bf16[32,8320]{1,0:T(8,128)(2,1)S(1)}, bf16[32,8320]{1,0:T(8,128)(2,1)S(1)}, u32[]{:S(2)}, u32[]{:S(2)}) collective-permute-start(bf16[32,8320]{1,0:T(8,128)(2,1)S(1)} %pick_rows.12), channel_id=1, source_target_pairs={{0,8},{8,0},{16,24},{24,16},{1,9},{9,1},{17,25},{25,17},{2,10},{10... | collective-permute-start | bytes 1597448 | tf_op jit(solution)/shard_map/ppermute | solution.py:18
  122.5 9.4 %collective-permute-start.28 = (bf16[32,4224]{1,0:T(8,128)(2,1)S(1)}, bf16[32,4224]{1,0:T(8,128)(2,1)S(1)}, u32[]{:S(2)}, u32[]{:S(2)}) collective-permute-start(bf16[32,4224]{1,0:T(8,128)(2,1)S(1)} %get-tuple-element.35), channel_id=1, source_target_pairs={{0,16},{8,24},{16,0},{24,8},{1,17},{9,25},{17,1},{25,9},{2,18},{10... | collective-permute-start | bytes 811016 | tf_op jit(solution)/shard_map/ppermute | solution.py:18
  123.0 13.7 %collective-permute-start.31 = (bf16[32,4224]{1,0:T(8,128)(2,1)S(1)}, bf16[32,4224]{1,0:T(8,128)(2,1)S(1)}, u32[]{:S(2)}, u32[]{:S(2)}) collective-permute-start(bf16[32,4224]{1,0:T(8,128)(2,1)S(1)} %get-tuple-element.38), channel_id=1, source_target_pairs={{0,24},{8,16},{16,8},{24,0},{1,25},{9,17},{17,9},{25,1},{2,26},{10... | collective-permute-start | bytes 811016 | tf_op jit(solution)/shard_map/ppermute | solution.py:18
  128.1 19.3 %collective-permute-start.29 = (bf16[32,2048]{1,0:T(8,128)(2,1)S(1)}, bf16[32,2048]{1,0:T(8,128)(2,1)S(1)}, u32[]{:S(2)}, u32[]{:S(2)}) collective-permute-start(bf16[32,2048]{1,0:T(8,128)(2,1)S(1)} %get-tuple-element.36), channel_id=1, source_target_pairs={{0,16},{8,24},{16,0},{24,8},{1,17},{9,25},{17,1},{25,9},{2,18},{10... | collective-permute-start | bytes 393224 | tf_op jit(solution)/shard_map/ppermute | solution.py:18
  128.7 18.8 %collective-permute-start.32 = (bf16[32,2048]{1,0:T(8,128)(2,1)S(1)}, bf16[32,2048]{1,0:T(8,128)(2,1)S(1)}, u32[]{:S(2)}, u32[]{:S(2)}) collective-permute-start(bf16[32,2048]{1,0:T(8,128)(2,1)S(1)} %get-tuple-element.39), channel_id=1, source_target_pairs={{0,24},{8,16},{16,8},{24,0},{1,25},{9,17},{17,9},{25,1},{2,26},{10... | collective-permute-start | bytes 393224 | tf_op jit(solution)/shard_map/ppermute | solution.py:18
  131.9 15.5 %collective-permute-start.30 = (bf16[32,2048]{1,0:T(8,128)(2,1)S(1)}, bf16[32,2048]{1,0:T(8,128)(2,1)S(1)}, u32[]{:S(2)}, u32[]{:S(2)}) collective-permute-start(bf16[32,2048]{1,0:T(8,128)(2,1)S(1)} %get-tuple-element.37), channel_id=1, source_target_pairs={{0,16},{8,24},{16,0},{24,8},{1,17},{9,25},{17,1},{25,9},{2,18},{10... | collective-permute-start | bytes 393224 | tf_op jit(solution)/shard_map/ppermute | solution.py:18
  136.7 11.2 %collective-permute-start.33 = (bf16[32,2048]{1,0:T(8,128)(2,1)S(1)}, bf16[32,2048]{1,0:T(8,128)(2,1)S(1)}, u32[]{:S(2)}, u32[]{:S(2)}) collective-permute-start(bf16[32,2048]{1,0:T(8,128)(2,1)S(1)} %get-tuple-element.40), channel_id=1, source_target_pairs={{0,24},{8,16},{16,8},{24,0},{1,25},{9,17},{17,9},{25,1},{2,26},{10... | collective-permute-start | bytes 393224 | tf_op jit(solution)/shard_map/ppermute | solution.py:18
  152.0 9.1 %collective-permute-start.34 = (bf16[32,1024]{1,0:T(8,128)(2,1)S(1)}, bf16[32,1024]{1,0:T(8,128)(2,1)S(1)}, u32[]{:S(2)}, u32[]{:S(2)}) collective-permute-start(bf16[32,1024]{1,0:T(8,128)(2,1)S(1)} %get-tuple-element.47), channel_id=1, source_target_pairs={{0,8},{8,0},{16,24},{24,16},{1,9},{9,1},{17,25},{25,17},{2,10},{10... | collective-permute-start | bytes 196616 | tf_op jit(solution)/shard_map/ppermute | solution.py:18
  152.4 8.7 %collective-permute-start.35 = (bf16[32,1024]{1,0:T(8,128)(2,1)S(1)}, bf16[32,1024]{1,0:T(8,128)(2,1)S(1)}, u32[]{:S(2)}, u32[]{:S(2)}) collective-permute-start(bf16[32,1024]{1,0:T(8,128)(2,1)S(1)} %get-tuple-element.46), channel_id=1, source_target_pairs={{0,16},{8,24},{16,0},{24,8},{1,17},{9,25},{17,1},{25,9},{2,18},{10... | collective-permute-start | bytes 196616 | tf_op jit(solution)/shard_map/ppermute | solution.py:18
  153.2 7.9 %collective-permute-start.36 = (bf16[32,1024]{1,0:T(8,128)(2,1)S(1)}, bf16[32,1024]{1,0:T(8,128)(2,1)S(1)}, u32[]{:S(2)}, u32[]{:S(2)}) collective-permute-start(bf16[32,1024]{1,0:T(8,128)(2,1)S(1)} %get-tuple-element.45), channel_id=1, source_target_pairs={{0,24},{8,16},{16,8},{24,0},{1,25},{9,17},{17,9},{25,1},{2,26},{10... | collective-permute-start | bytes 196616 | tf_op jit(solution)/shard_map/ppermute | solution.py:18

commit v2 on v1

--- a/solution.py
+++ b/solution.py
@@ -69,15 +69,15 @@
     return total
 
 
-def early_kernel(part, has_prior, tile, ids_ref, *refs):
-    xs = refs[: len(part)]
-    anchor_ref = refs[len(part)]
-    prior = refs[len(part) + 1 : -1]
-    sum_ref = refs[-1]
+def early_kernel(squared, has_prior, n_part, tile, ids_ref, *refs):
+    xs = refs[:n_part]
+    anchor_ref, inverse_ref = refs[n_part : n_part + 2]
+    prior = refs[n_part + 2 : -2]
+    sum_ref, square_ref = refs[-2:]
     step = pl.program_id(0)
     width = anchor_ref.shape[2]
     cols = min(2 * tile, width)
-    for k in range(len(part)):
+    for k in range(n_part):
 
         @pl.when(step == k)
         def _(k=k):
@@ -91,28 +91,41 @@
                     value += prior[0][:, lanes]
                 sum_ref[:, lanes] = value
 
-
-def early_products(row_of, part, xs, anchor, prior, layer, tile):
+    @pl.when(step == 0)
+    def _():
+        squares = prior[1][...] if has_prior else jnp.zeros(square_ref.shape, F32)
+        for k, p in squared:
+            x_ref = xs[k]
+            squares = square_sum(squares, x_ref, inverse_ref, p, tile)
+        square_ref[...] = squares
+
+
+def early_products(row_of, xs, n_part, squared, anchor, inverse, prior, layer, tile):
     rows, width = xs[0].shape
+    whole_rows = pl.BlockSpec((rows, width), lambda i, ids: (0, 0))
+    whole_tile = pl.BlockSpec((rows, tile), lambda i, ids: (0, 0))
     return pl.pallas_call(
-        functools.partial(early_kernel, part, bool(prior), tile),
-        out_shape=jax.ShapeDtypeStruct((rows, width), F32),
+        functools.partial(early_kernel, squared, bool(prior), n_part, tile),
+        out_shape=[
+            jax.ShapeDtypeStruct((rows, width), F32),
+            jax.ShapeDtypeStruct((rows, tile), F32),
+        ],
         grid_spec=pltpu.PrefetchScalarGridSpec(
             num_scalar_prefetch=1,
-            grid=(len(part),),
-            in_specs=[whole()] * len(part)
+            grid=(n_part,),
+            in_specs=[whole()] * len(xs)
             + [pl.BlockSpec((1, width, width), lambda i, ids: (layer, ids[i], 0))]
-            + [whole()] * len(prior),
-            out_specs=pl.BlockSpec((rows, width), lambda i, ids: (0, 0)),
+            + [whole()] * (1 + len(prior)),
+            out_specs=[whole_rows, whole_tile],
         ),
         compiler_params=params(32, dimension_semantics=("arbitrary",)),
         cost_estimate=pl.CostEstimate(
-            flops=2 * rows * width * width * len(part),
-            bytes_accessed=2 * width * width * len(part),
+            flops=2 * rows * width * width * n_part,
+            bytes_accessed=2 * width * width * n_part,
             transcendentals=0,
         ),
         name="early_products",
-    )(row_of, *xs, anchor, *prior)
+    )(row_of, *xs, anchor, inverse, *prior)
 
 
 def stage_kernel(layer, tiles_ref, out_ref, sem):
@@ -143,7 +156,7 @@
 
 
 def product_kernel(cfg, ids_ref, *refs):
-    n_in, plan, label_plan, parts, has_prior, layer, n_cols, col_step, width = cfg
+    n_in, plan, label_plan, parts, has_prior, done, layer, n_cols, col_step, width = cfg
     src = refs[:n_in]
     tiles_ref = refs[n_in]
     at = n_in + 1
@@ -152,8 +165,8 @@
         anchor_ref, stream_ref, inverse_ref = refs[at : at + 3]
         at += 3
         if has_prior:
-            sum_ref = refs[at]
-            at += 1
+            sum_ref, square_ref = refs[at : at + 2]
+            at += 2
         out_ref, scale_ref = refs[at : at + 2]
         at += 2
     else:
@@ -210,9 +223,10 @@
     for t in range(n_slots):
         masks[t] = jnp.where(label == t + 1, 1.0, 0.0).astype(BF16)
     if with_anchor:
-        squares = jnp.zeros((rows, tile), F32)
+        squares = square_ref[...] if has_prior else jnp.zeros((rows, tile), F32)
         for p in range(shards):
-            squares = square_sum(squares, full.at[p], inverse_ref, p, tile)
+            if p not in done:
+                squares = square_sum(squares, full.at[p], inverse_ref, p, tile)
         mean = jnp.sum(squares, axis=1, keepdims=True) / (width * shards)
         scale_ref[...] = jnp.broadcast_to(lax.rsqrt(mean + EPS), (rows, tile))
         for copy in weights:
@@ -231,7 +245,8 @@
                 anchor_out += sum_ref[:, lanes]
             for k in range(0, step_cols, tile):
                 out = anchor_out[:, k : k + tile] * scale_ref[...]
-                out_ref[:, n + k : n + k + tile] = stream_ref[:, n + k : n + k + tile] + out
+                here = slice(n + k, n + k + tile)
+                out_ref[:, here] = stream_ref[:, here].astype(F32) + out
 
     def block_step(step, carry):
         for k in range(col_step):
@@ -261,14 +276,14 @@
 
 def products(
     ids, sources, plan, label_plan, rows, tiles, layer, col_step,
-    parts=None, anchor=None, stream=None, inverse=None, prior=(),
+    parts=None, anchor=None, stream=None, inverse=None, prior=(), done=(),
 ):
     n_slots, n_cols, per_list, tile, _ = tiles.shape
     shards = 1 + max(place[1] for places in plan for place in places)
     width = n_cols * tile
     with_anchor = parts is not None
     cfg = (
-        len(sources), plan, label_plan, parts, bool(prior), layer, n_cols, col_step, width,
+        len(sources), plan, label_plan, parts, bool(prior), done, layer, n_cols, col_step, width,
     )
     in_specs = [in_place()] * len(sources) + [whole()]
     operands = [*sources, tiles]
@@ -305,6 +320,21 @@
     )(ids, *operands)
 
 
+def first_kernel(hidden_ref, gain_ref, y_ref):
+    y_ref[...] = (hidden_ref[...].astype(F32) * gain_ref[0:1, :]).astype(BF16)
+
+
+def first_rows(hidden, norm_gain):
+    return pl.pallas_call(
+        first_kernel,
+        out_shape=jax.ShapeDtypeStruct(hidden.shape, BF16),
+        in_specs=[whole()] * 2,
+        out_specs=whole(),
+        compiler_params=params(8),
+        name="first_rows",
+    )(hidden, norm_gain)
+
+
 def join_kernel(n_dest, last, *refs):
     partial_ref, back_ref, scale_ref = refs[:3]
     rets = refs[3 : 3 + n_dest]
@@ -381,8 +411,8 @@
     offsets = list(range(1, groups))
     pairwise = tp_count == 8
 
-    stream = hidden.astype(F32)
-    y = (stream * norm_gain[0][None, :]).astype(BF16)
+    stream = hidden
+    y = first_rows(hidden, norm_gain)
 
     owner = tenant // per_group
     local = tenant % per_group
@@ -449,18 +479,20 @@
         for pieces in far[1:]:
             got += pieces
         tiles = stage_tiles(delta_tiles, layer)
-        prior = ()
+        prior, done = (), ()
         for part in early:
             row_of = jnp.stack([jnp.bitwise_xor(base, p) for p in part])
+            squared = tuple(enumerate(part)) if layer > 0 else ()
             prior = early_products(
-                row_of, part, [shards[p] for p in part], anchor, prior, layer, tile
+                row_of, [shards[p] for p in part], len(part), squared, anchor,
+                inverse[layer] if layer > 0 else norm_gain, prior, layer, tile,
             )
-            prior = (prior,)
+            done += tuple(p for _, p in squared)
         partial, scale = products(
             ids, shards + [own_label], own_plan, own_labels, rows, tiles,
             layer, 2,
             parts=late, anchor=anchor, stream=stream, inverse=inverse[layer],
-            prior=prior,
+            prior=tuple(prior), done=done,
         )
         answers = products(
             ids, got, sent_plan, sent_labels, n_dest * cap, tiles, layer, 2

time: 163 us -> 162 us (level)
  other arithmetic: 5.06 us -> 3.08 us
    convert_element_type x2 -> x0, other arithmetic: 1.99 us -> none  [the longest x1 1 us: body(): y = (stream * norm_gain[0][None, :]).astype(BF16)]
    unnamed x6 -> x14, local copies, waits for them, and re-layouts: 3.29 us -> 4.96 us
    pallas_call x6 -> x7, Pallas kernels: 20.3 us -> 20.3 us  [the longest x6 20.3 us: early_products(): pl.pallas_call(functools.partial(early_kernel, squared, bool(prior), n_pa...]
  transfers between devices with their start and end apart: 37 -> 37, of which waited for: 12 -> 12; matrix products, arithmetic and copies ran while one was open for 4% -> 3% of each run, Pallas kernels for 27% -> 27%
where the time goes in v2:
time: 162 us; the launch traced here: 161 us
  waiting for transfers between devices  61.3 us (38%)
  Pallas kernels  53.5 us (33%)
  starting transfers between devices  36.1 us (22%)
  local copies, waits for them, and re-layouts  6.63 us (4%)
  other arithmetic  3.08 us (2%)
    ppermute x37, waiting for transfers between devices, swap(): return lax.ppermute(value, axis, [(i, i ^ offset) for i in range(size)])  61.3 us
    ppermute x37, starting transfers between devices, swap(): return lax.ppermute(value, axis, [(i, i ^ offset) for i in range(size)])  36.1 us
    pallas_call x4, Pallas kernels, products(): pl.pallas_call(functools.partial(product_kernel, cfg), out_shape=out_shap...  22.3 us
    pallas_call x6, Pallas kernels, early_products(): pl.pallas_call(functools.partial(early_kernel, squared, bool(prior), n_pa...  20.3 us
    pallas_call x2, Pallas kernels, stage_tiles(): pl.pallas_call(functools.partial(stage_kernel, layer), out_shape=jax.Shap...  6.94 us
    unnamed x14, local copies, waits for them, and re-layouts  4.96 us
  transfers between devices with their start and end apart: 37, of which 12 were waited for; matrix products, arithmetic and copies ran while one was open for 3% of the time, Pallas kernels for 27%

profile of v2, /device:TPU:0, one launch (start us, length us, event | category | flops | bytes accessed | tf_op | source)
XLA Modules:
  0.0 161.1 jit_solution(12586008733834733076)
XLA Ops:
  0.0 0.9 copy-done.1
  1.0 0.7 copy-done.3
  1.7 3.1 %collective-permute-start = (bf16[128,1024]{1,0:T(8,128)(2,1)S(1)}, bf16[128,1024]{1,0:T(8,128)(2,1)S(1)}, u32[]{:S(2)}, u32[]{:S(2)}) collective-permute-start(bf16[128,1024]{1,0:T(8,128)(2,1)S(1)} %first_rows.1.refs_0_.refs_1_), channel_id=1, source_target_pairs={{0,1},{1,0},{2,3},{3,2},{4,5},{5,4},{6,7},{7,6},{8,9},{9,8},{10,11... | collective-permute-start | bytes 786440 | tf_op jit(solution)/shard_map/ppermute | solution.py:18
  4.8 1.6 collective-permute-start.1
  6.3 2.6 %collective-permute-start.3 = (bf16[128,1024]{1,0:T(8,128)(2,1)S(1)}, bf16[128,1024]{1,0:T(8,128)(2,1)S(1)}, u32[]{:S(2)}, u32[]{:S(2)}) collective-permute-start(bf16[128,1024]{1,0:T(8,128)(2,1)S(1)} %first_rows.1.refs_0_.refs_1_), channel_id=1, source_target_pairs={{0,4},{1,5},{2,6},{3,7},{4,0},{5,1},{6,2},{7,3},{8,12},{9,13},{10,... | collective-permute-start | bytes 786440 | tf_op jit(solution)/shard_map/ppermute | solution.py:18
  11.2 0.8 select_bitcast_fusion
  12.8 7.6 %collective-permute-done.3.refs_1_.refs_4_.refs_5_ = bf16[128,1024]{1,0:T(8,128)(2,1)S(1)} collective-permute-done((bf16[128,1024]{1,0:T(8,128)(2,1)S(1)}, bf16[128,1024]{1,0:T(8,128)(2,1)S(1)}, u32[]{:S(2)}, u32[]{:S(2)}) %collective-permute-start.3) | collective-permute-done | bytes 262176 | tf_op jit(solution)/shard_map/ppermute | solution.py:18
  21.5 1.5 collective-permute-start.2
  23.1 4.8 %collective-permute-done.4.refs_0_.refs_5_.refs_6_.refs_1_ = bf16[128,1024]{1,0:T(8,128)(2,1)S(1)} collective-permute-done((bf16[128,1024]{1,0:T(8,128)(2,1)S(1)}, bf16[128,1024]{1,0:T(8,128)(2,1)S(1)}, u32[]{:S(2)}, u32[]{:S(2)}) %collective-permute-start.4) | collective-permute-done | bytes 262176 | tf_op jit(solution)/shard_map/ppermute | solution.py:18
  27.8 2.2 %collective-permute-start.6 = (bf16[128,1024]{1,0:T(8,128)(2,1)S(1)}, bf16[128,1024]{1,0:T(8,128)(2,1)S(1)}, u32[]{:S(2)}, u32[]{:S(2)}) collective-permute-start(bf16[128,1024]{1,0:T(8,128)(2,1)S(1)} %collective-permute-done.4.refs_0_.refs_5_.refs_6_.refs_1_), channel_id=1, source_target_pairs={{0,2},{1,3},{2,0},{3,1},{4,6},{5,7},{6,4},{7,5},{8,10},{9,11},{10,... | collective-permute-start | bytes 786440 | tf_op jit(solution)/shard_map/ppermute | solution.py:18
  30.3 4.6 %collective-permute-done.8 = f32[2,2,1024]{2,1,0:T(2,128)S(1)} collective-permute-done((f32[2,2,1024]{2,1,0:T(2,128)S(1)}, f32[2,2,1024]{2,1,0:T(2,128)S(1)}, u32[]{:S(2)}, u32[]{:S(2)}) %collective-permute-start.8) | collective-permute-done | bytes 16416 | tf_op jit(solution)/shard_map/ppermute | solution.py:18
  34.9 2.0 %collective-permute-start.9 = (f32[2,4,1024]{2,1,0:T(4,128)S(1)}, f32[2,4,1024]{2,1,0:T(4,128)S(1)}, u32[]{:S(2)}, u32[]{:S(2)}) collective-permute-start(f32[2,4,1024]{2,1,0:T(4,128)S(1)} %pad_maximum_fusion), channel_id=1, source_target_pairs={{0,4},{1,5},{2,6},{3,7},{4,0},{5,1},{6,2},{7,3},{8,12},{9,13},{10,... | collective-permute-start | bytes 98312 | tf_op jit(solution)/shard_map/ppermute | solution.py:18
  37.7 0.7 slice.56.refs_6_
  38.4 3.5 %stage_tiles.2.refs_9_.refs_7_ = bf16[8,8,4,128,128]{4,3,2,1,0:T(8,128)(2,1)S(1)} custom-call(bf16[8,2,8,4,128,128]{5,4,3,2,1,0:T(8,128)(2,1)} %tiles_ref.3), custom_call_target="tpu_custom_call" | custom-call | bytes 16777216 | tf_op jit(solution)/shard_map/stage_tiles/pallas_call | solution.py:144
  41.9 3.3 %copy-done = bf16[8,8,4,128,128]{4,3,2,1,0:T(8,128)(2,1)} copy-done((bf16[8,8,4,128,128]{4,3,2,1,0:T(8,128)(2,1)}, bf16[8,8,4,128,128]{4,3,2,1,0:T(8,128)(2,1)S(1)}, u32[]{:S(2)}) %copy-start) | copy-done | bytes 8388632
  45.6 1.6 collective-permute-start.11
  47.8 1.6 collective-permute-start.12
  49.7 5.3 %collective-permute-done.11.refs_1_ = bf16[32,4224]{1,0:T(8,128)(2,1)S(1)} collective-permute-done((bf16[32,4224]{1,0:T(8,128)(2,1)S(1)}, bf16[32,4224]{1,0:T(8,128)(2,1)S(1)}, u32[]{:S(2)}, u32[]{:S(2)}) %collective-permute-start.11) | collective-permute-done | bytes 270368 | tf_op jit(solution)/shard_map/ppermute | solution.py:18
  55.0 1.5 collective-permute-start.13
  56.5 3.3 %collective-permute-done.14.refs_4_ = bf16[32,4224]{1,0:T(8,128)(2,1)S(1)} collective-permute-done((bf16[32,4224]{1,0:T(8,128)(2,1)S(1)}, bf16[32,4224]{1,0:T(8,128)(2,1)S(1)}, u32[]{:S(2)}, u32[]{:S(2)}) %collective-permute-start.14) | collective-permute-done | bytes 270368 | tf_op jit(solution)/shard_map/ppermute | solution.py:18
  59.8 1.9 %collective-permute-start.16 = (bf16[32,2048]{1,0:T(8,128)(2,1)S(1)}, bf16[32,2048]{1,0:T(8,128)(2,1)S(1)}, u32[]{:S(2)}, u32[]{:S(2)}) collective-permute-start(bf16[32,2048]{1,0:T(8,128)(2,1)S(1)} %get-tuple-element.48), channel_id=1, source_target_pairs={{0,24},{8,16},{16,8},{24,0},{1,25},{9,17},{17,9},{25,1},{2,26},{10... | collective-permute-start | bytes 393224 | tf_op jit(solution)/shard_map/ppermute | solution.py:18
  61.7 3.4 %early_products.6 = (f32[128,1024]{1,0:T(8,128)S(1)}, f32[128,128]{1,0:T(8,128)S(1)}) custom-call(s32[2]{0:T(128)S(1)} %pad_add_fusion.3.ids_ref, bf16[128,1024]{1,0:T(8,128)(2,1)S(1)} %first_rows.1.refs_0_.refs_1_, bf16[128,1024]{1,0:T(8,128)(2,1)S(1)} %collective-permute-done.refs_1_.refs_2_, bf16[2,8192,1024]{2,1,0:T(8,128)(2,1)} %refs_10_.3, ...), custom_call_target="tpu_custom_call" | custom-call | flops 536870912 | bytes 4194304 | tf_op jit(solution)/shard_map/early_products/pallas_call | solution.py:107
  65.1 3.5 %early_products.7 = (f32[128,1024]{1,0:T(8,128)S(1)}, f32[128,128]{1,0:T(8,128)S(1)}) custom-call(s32[2]{0:T(128)S(1)} %pad_add_fusion.2.ids_ref, bf16[128,1024]{1,0:T(8,128)(2,1)S(1)} %collective-permute-done.1.refs_0_.refs_2_.refs_3_, bf16[128,1024]{1,0:T(8,128)(2,1)S(1)} %collective-permute-done.3.refs_1_.refs_4_.refs_5_, ...), custom_call_target="tpu_custom_call" | custom-call | flops 536870912 | bytes 4194304 | tf_op jit(solution)/shard_map/early_products/pallas_call | solution.py:107
  68.7 3.5 %early_products.8 = (f32[128,1024]{1,0:T(8,128)S(1)}, f32[128,128]{1,0:T(8,128)S(1)}) custom-call(s32[2]{0:T(128)S(1)} %pad_add_fusion.1.ids_ref, bf16[128,1024]{1,0:T(8,128)(2,1)S(1)} %collective-permute-done.4.refs_0_.refs_5_.refs_6_.refs_1_, bf16[128,1024]{1,0:T(8,128)(2,1)S(1)} %collective-permute-done.5.refs_1_.refs_6_.refs_7_.refs_2_, ...), custom_call_target="tpu_custom_call" | custom-call | flops 536870912 | bytes 4194304 | tf_op jit(solution)/shard_map/early_products/pallas_call | solution.py:107
  72.3 4.1 %sent_products.2 = bf16[96,1024]{1,0:T(8,128)(2,1)S(1)} custom-call(s32[264]{0:T(512)S(1)} %get-tuple-element.65.ids_ref, bf16[32,8320]{1,0:T(8,128)(2,1)S(1)} %collective-permute-done.10.refs_0_, bf16[32,4224]{1,0:T(8,128)(2,1)S(1)} %collective-permute-done.11.refs_1_, bf16[32,2048]{1,0:T(8,128)(2,1)S(1)} %collective-permute-done.12.refs_2_, ...), custom_call_target="tpu_custom_call" | custom-call | flops 805306368 | bytes 9961472 | tf_op jit(solution)/shard_map/sent_products/pallas_call | solution.py:311
  77.1 1.3 collective-permute-start.19
  78.3 7.1 %own_products.2 = (f32[128,1024]{1,0:T(8,128)S(1)}, f32[128,128]{1,0:T(8,128)S(1)}) custom-call(s32[264]{0:T(512)S(1)} %get-tuple-element.65.ids_ref, bf16[128,1024]{1,0:T(8,128)(2,1)S(1)} %first_rows.1.refs_0_.refs_1_, bf16[128,1024]{1,0:T(8,128)(2,1)S(1)} %collective-permute-done.refs_1_.refs_2_, ...), custom_call_target="tpu_custom_call" | custom-call | flops 1610612736 | bytes 14680064 | tf_op jit(solution)/shard_map/own_products/pallas_call | solution.py:311
  86.0 1.0 collective-permute-start.23
  87.0 2.1 %collective-permute-start.21 = (bf16[128,1024]{1,0:T(8,128)(2,1)S(1)}, bf16[128,1024]{1,0:T(8,128)(2,1)S(1)}, u32[]{:S(2)}, u32[]{:S(2)}) collective-permute-start(bf16[128,1024]{1,0:T(8,128)(2,1)S(1)} %get-tuple-element.49.refs_0_.refs_1_), channel_id=1, source_target_pairs={{0,2},{1,3},{2,0},{3,1},{4,6},{5,7},{6,4},{7,5},{8,10},{9,11},{10,... | collective-permute-start | bytes 786440 | tf_op jit(solution)/shard_map/ppermute | solution.py:18
  89.1 12.0 %collective-permute-done.23.refs_1_.refs_4_.refs_5_ = bf16[128,1024]{1,0:T(8,128)(2,1)S(1)} collective-permute-done((bf16[128,1024]{1,0:T(8,128)(2,1)S(1)}, bf16[128,1024]{1,0:T(8,128)(2,1)S(1)}, u32[]{:S(2)}, u32[]{:S(2)}) %collective-permute-start.23) | collective-permute-done | bytes 262176 | tf_op jit(solution)/shard_map/ppermute | solution.py:18
  101.6 1.5 collective-permute-start.20
  103.7 6.6 %collective-permute-done.24.refs_0_.refs_5_.refs_6_.refs_1_ = bf16[128,1024]{1,0:T(8,128)(2,1)S(1)} collective-permute-done((bf16[128,1024]{1,0:T(8,128)(2,1)S(1)}, bf16[128,1024]{1,0:T(8,128)(2,1)S(1)}, u32[]{:S(2)}, u32[]{:S(2)}) %collective-permute-start.24) | collective-permute-done | bytes 262176 | tf_op jit(solution)/shard_map/ppermute | solution.py:18
  110.2 5.6 %collective-permute-done.20.refs_1_.refs_2_ = bf16[128,1024]{1,0:T(8,128)(2,1)S(1)} collective-permute-done((bf16[128,1024]{1,0:T(8,128)(2,1)S(1)}, bf16[128,1024]{1,0:T(8,128)(2,1)S(1)}, u32[]{:S(2)}, u32[]{:S(2)}) %collective-permute-start.20) | collective-permute-done | bytes 262176 | tf_op jit(solution)/shard_map/ppermute | solution.py:18
  115.9 4.6 %collective-permute-done.22.refs_3_.refs_4_.refs_1_ = bf16[128,1024]{1,0:T(8,128)(2,1)S(1)} collective-permute-done((bf16[128,1024]{1,0:T(8,128)(2,1)S(1)}, bf16[128,1024]{1,0:T(8,128)(2,1)S(1)}, u32[]{:S(2)}, u32[]{:S(2)}) %collective-permute-start.22) | collective-permute-done | bytes 262176 | tf_op jit(solution)/shard_map/ppermute | solution.py:18
  121.9 1.4 collective-permute-start.31
  123.2 3.5 %stage_tiles.3.refs_9_.refs_7_ = bf16[8,8,4,128,128]{4,3,2,1,0:T(8,128)(2,1)S(1)} custom-call(bf16[8,2,8,4,128,128]{5,4,3,2,1,0:T(8,128)(2,1)} %tiles_ref.3), custom_call_target="tpu_custom_call" | custom-call | bytes 16777216 | tf_op jit(solution)/shard_map/stage_tiles/pallas_call | solution.py:144
  127.5 1.2 collective-permute-start.32
  128.9 1.9 %collective-permute-done.28.refs_1_ = bf16[32,4224]{1,0:T(8,128)(2,1)S(1)} collective-permute-done((bf16[32,4224]{1,0:T(8,128)(2,1)S(1)}, bf16[32,4224]{1,0:T(8,128)(2,1)S(1)}, u32[]{:S(2)}, u32[]{:S(2)}) %collective-permute-start.28) | collective-permute-done | bytes 270368 | tf_op jit(solution)/shard_map/ppermute | solution.py:18
  131.2 4.4 %collective-permute-done.31.refs_4_ = bf16[32,4224]{1,0:T(8,128)(2,1)S(1)} collective-permute-done((bf16[32,4224]{1,0:T(8,128)(2,1)S(1)}, bf16[32,4224]{1,0:T(8,128)(2,1)S(1)}, u32[]{:S(2)}, u32[]{:S(2)}) %collective-permute-start.31) | collective-permute-done | bytes 270368 | tf_op jit(solution)/shard_map/ppermute | solution.py:18
  135.6 0.9 collective-permute-start.33
  136.5 3.3 %early_products.9 = (f32[128,1024]{1,0:T(8,128)S(1)}, f32[128,128]{1,0:T(8,128)S(1)}) custom-call(s32[2]{0:T(128)S(1)} %pad_add_fusion.3.ids_ref, bf16[128,1024]{1,0:T(8,128)(2,1)S(1)} %get-tuple-element.49.refs_0_.refs_1_, bf16[128,1024]{1,0:T(8,128)(2,1)S(1)} %collective-permute-done.20.refs_1_.refs_2_, bf16[2,8192,1024]{2,1,0:T(8,128)(2,1)} %refs_10_.3, ...), custom_call_target="tpu_custom_call" | custom-call | flops 536870912 | bytes 4194304 | tf_op jit(solution)/shard_map/early_products/pallas_call | solution.py:107
  139.7 3.3 %early_products.10 = (f32[128,1024]{1,0:T(8,128)S(1)}, f32[128,128]{1,0:T(8,128)S(1)}) custom-call(s32[2]{0:T(128)S(1)} %pad_add_fusion.2.ids_ref, bf16[128,1024]{1,0:T(8,128)(2,1)S(1)} %collective-permute-done.21.refs_0_.refs_2_.refs_3_, bf16[128,1024]{1,0:T(8,128)(2,1)S(1)} %collective-permute-done.23.refs_1_.refs_4_.refs_5_, ...), custom_call_target="tpu_custom_call" | custom-call | flops 536870912 | bytes 4194304 | tf_op jit(solution)/shard_map/early_products/pallas_call | solution.py:107
  143.0 3.3 %early_products.11 = (f32[128,1024]{1,0:T(8,128)S(1)}, f32[128,128]{1,0:T(8,128)S(1)}) custom-call(s32[2]{0:T(128)S(1)} %pad_add_fusion.1.ids_ref, bf16[128,1024]{1,0:T(8,128)(2,1)S(1)} %collective-permute-done.24.refs_0_.refs_5_.refs_6_.refs_1_, bf16[128,1024]{1,0:T(8,128)(2,1)S(1)} %collective-permute-done.25.refs_1_.refs_6_.refs_7_.refs_2_, ...), custom_call_target="tpu_custom_call" | custom-call | flops 536870912 | bytes 4194304 | tf_op jit(solution)/shard_map/early_products/pallas_call | solution.py:107
  146.8 4.0 %sent_products.3 = bf16[96,1024]{1,0:T(8,128)(2,1)S(1)} custom-call(s32[264]{0:T(512)S(1)} %get-tuple-element.66.ids_ref, bf16[32,8320]{1,0:T(8,128)(2,1)S(1)} %collective-permute-done.27.refs_0_, bf16[32,4224]{1,0:T(8,128)(2,1)S(1)} %collective-permute-done.28.refs_1_, bf16[32,2048]{1,0:T(8,128)(2,1)S(1)} %collective-permute-done.29.refs_2_, ...), custom_call_target="tpu_custom_call" | custom-call | flops 805306368 | bytes 9961472 | tf_op jit(solution)/shard_map/sent_products/pallas_call | solution.py:311
  151.3 0.8 collective-permute-start.35
  152.1 0.8 collective-permute-start.36
  152.8 7.1 %own_products.3 = (f32[128,1024]{1,0:T(8,128)S(1)}, f32[128,128]{1,0:T(8,128)S(1)}) custom-call(s32[264]{0:T(512)S(1)} %get-tuple-element.66.ids_ref, bf16[128,1024]{1,0:T(8,128)(2,1)S(1)} %get-tuple-element.49.refs_0_.refs_1_, bf16[128,1024]{1,0:T(8,128)(2,1)S(1)} %collective-permute-done.20.refs_1_.refs_2_, ...), custom_call_target="tpu_custom_call" | custom-call | flops 1610612736 | bytes 14680064 | tf_op jit(solution)/shard_map/own_products/pallas_call | solution.py:311
  160.0 1.1 join.3
  (100 shorter events, 12.7 us)
Async XLA Ops:
  0.0 0.9 copy-start.1
  1.0 0.7 copy-start.3
  1.6 60.0 %copy-start.4 = (f32[2,1024]{1,0:T(2,128)S(1)}, f32[2,1024]{1,0:T(2,128)}, u32[]{:S(2)}) copy-start(f32[2,1024]{1,0:T(2,128)} %refs_3_.5) | copy-start | bytes 24580
  1.7 35.2 %collective-permute-start = (bf16[128,1024]{1,0:T(8,128)(2,1)S(1)}, bf16[128,1024]{1,0:T(8,128)(2,1)S(1)}, u32[]{:S(2)}, u32[]{:S(2)}) collective-permute-start(bf16[128,1024]{1,0:T(8,128)(2,1)S(1)} %first_rows.1.refs_0_.refs_1_), channel_id=1, source_target_pairs={{0,1},{1,0},{2,3},{3,2},{4,5},{5,4},{6,7},{7,6},{8,9},{9,8},{10,11... | collective-permute-start | bytes 786440 | tf_op jit(solution)/shard_map/ppermute | solution.py:18
  4.8 16.8 %collective-permute-start.1 = (bf16[128,1024]{1,0:T(8,128)(2,1)S(1)}, bf16[128,1024]{1,0:T(8,128)(2,1)S(1)}, u32[]{:S(2)}, u32[]{:S(2)}) collective-permute-start(bf16[128,1024]{1,0:T(8,128)(2,1)S(1)} %first_rows.1.refs_0_.refs_1_), channel_id=1, source_target_pairs={{0,2},{1,3},{2,0},{3,1},{4,6},{5,7},{6,4},{7,5},{8,10},{9,11},{10,... | collective-permute-start | bytes 786440 | tf_op jit(solution)/shard_map/ppermute | solution.py:18
  6.3 14.0 %collective-permute-start.3 = (bf16[128,1024]{1,0:T(8,128)(2,1)S(1)}, bf16[128,1024]{1,0:T(8,128)(2,1)S(1)}, u32[]{:S(2)}, u32[]{:S(2)}) collective-permute-start(bf16[128,1024]{1,0:T(8,128)(2,1)S(1)} %first_rows.1.refs_0_.refs_1_), channel_id=1, source_target_pairs={{0,4},{1,5},{2,6},{3,7},{4,0},{5,1},{6,2},{7,3},{8,12},{9,13},{10,... | collective-permute-start | bytes 786440 | tf_op jit(solution)/shard_map/ppermute | solution.py:18
  8.9 21.1 %collective-permute-start.7 = (f32[2,1,1024]{2,1,0:T(1,128)S(1)}, f32[2,1,1024]{2,1,0:T(1,128)S(1)}, u32[]{:S(2)}, u32[]{:S(2)}) collective-permute-start(f32[2,1,1024]{2,1,0:T(1,128)S(1)} %broadcast_in_dim.24), channel_id=1, source_target_pairs={{0,1},{1,0},{2,3},{3,2},{4,5},{5,4},{6,7},{7,6},{8,9},{9,8},{10,11... | collective-permute-start | bytes 24584 | tf_op jit(solution)/shard_map/ppermute | solution.py:18
  20.4 7.4 %collective-permute-start.4 = (bf16[128,1024]{1,0:T(8,128)(2,1)S(1)}, bf16[128,1024]{1,0:T(8,128)(2,1)S(1)}, u32[]{:S(2)}, u32[]{:S(2)}) collective-permute-start(bf16[128,1024]{1,0:T(8,128)(2,1)S(1)} %collective-permute-done.3.refs_1_.refs_4_.refs_5_), channel_id=1, source_target_pairs={{0,1},{1,0},{2,3},{3,2},{4,5},{5,4},{6,7},{7,6},{8,9},{9,8},{10,11... | collective-permute-start | bytes 786440 | tf_op jit(solution)/shard_map/ppermute | solution.py:18
  21.1 15.8 %collective-permute-start.5 = (bf16[128,1024]{1,0:T(8,128)(2,1)S(1)}, bf16[128,1024]{1,0:T(8,128)(2,1)S(1)}, u32[]{:S(2)}, u32[]{:S(2)}) collective-permute-start(bf16[128,1024]{1,0:T(8,128)(2,1)S(1)} %collective-permute-done.3.refs_1_.refs_4_.refs_5_), channel_id=1, source_target_pairs={{0,2},{1,3},{2,0},{3,1},{4,6},{5,7},{6,4},{7,5},{8,10},{9,11},{10,... | collective-permute-start | bytes 786440 | tf_op jit(solution)/shard_map/ppermute | solution.py:18
  21.5 15.4 %collective-permute-start.2 = (bf16[128,1024]{1,0:T(8,128)(2,1)S(1)}, bf16[128,1024]{1,0:T(8,128)(2,1)S(1)}, u32[]{:S(2)}, u32[]{:S(2)}) collective-permute-start(bf16[128,1024]{1,0:T(8,128)(2,1)S(1)} %collective-permute-done.1.refs_0_.refs_2_.refs_3_), channel_id=1, source_target_pairs={{0,1},{1,0},{2,3},{3,2},{4,5},{5,4},{6,7},{7,6},{8,9},{9,8},{10,11... | collective-permute-start | bytes 786440 | tf_op jit(solution)/shard_map/ppermute | solution.py:18
  27.8 9.1 %collective-permute-start.6 = (bf16[128,1024]{1,0:T(8,128)(2,1)S(1)}, bf16[128,1024]{1,0:T(8,128)(2,1)S(1)}, u32[]{:S(2)}, u32[]{:S(2)}) collective-permute-start(bf16[128,1024]{1,0:T(8,128)(2,1)S(1)} %collective-permute-done.4.refs_0_.refs_5_.refs_6_.refs_1_), channel_id=1, source_target_pairs={{0,2},{1,3},{2,0},{3,1},{4,6},{5,7},{6,4},{7,5},{8,10},{9,11},{10,... | collective-permute-start | bytes 786440 | tf_op jit(solution)/shard_map/ppermute | solution.py:18
  30.0 4.9 %collective-permute-start.8 = (f32[2,2,1024]{2,1,0:T(2,128)S(1)}, f32[2,2,1024]{2,1,0:T(2,128)S(1)}, u32[]{:S(2)}, u32[]{:S(2)}) collective-permute-start(f32[2,2,1024]{2,1,0:T(2,128)S(1)} %pad_maximum_fusion.1), channel_id=1, source_target_pairs={{0,2},{1,3},{2,0},{3,1},{4,6},{5,7},{6,4},{7,5},{8,10},{9,11},{10,... | collective-permute-start | bytes 49160 | tf_op jit(solution)/shard_map/ppermute | solution.py:18
  34.9 12.6 %collective-permute-start.9 = (f32[2,4,1024]{2,1,0:T(4,128)S(1)}, f32[2,4,1024]{2,1,0:T(4,128)S(1)}, u32[]{:S(2)}, u32[]{:S(2)}) collective-permute-start(f32[2,4,1024]{2,1,0:T(4,128)S(1)} %pad_maximum_fusion), channel_id=1, source_target_pairs={{0,4},{1,5},{2,6},{3,7},{4,0},{5,1},{6,2},{7,3},{8,12},{9,13},{10,... | collective-permute-start | bytes 98312 | tf_op jit(solution)/shard_map/ppermute | solution.py:18
  37.4 34.9 %collective-permute-start.10 = (bf16[32,8320]{1,0:T(8,128)(2,1)S(1)}, bf16[32,8320]{1,0:T(8,128)(2,1)S(1)}, u32[]{:S(2)}, u32[]{:S(2)}) collective-permute-start(bf16[32,8320]{1,0:T(8,128)(2,1)S(1)} %pick_rows.8), channel_id=1, source_target_pairs={{0,8},{8,0},{16,24},{24,16},{1,9},{9,1},{17,25},{25,17},{2,10},{10... | collective-permute-start | bytes 1597448 | tf_op jit(solution)/shard_map/ppermute | solution.py:18
  41.9 3.3 %copy-start = (bf16[8,8,4,128,128]{4,3,2,1,0:T(8,128)(2,1)}, bf16[8,8,4,128,128]{4,3,2,1,0:T(8,128)(2,1)S(1)}, u32[]{:S(2)}) copy-start(bf16[8,8,4,128,128]{4,3,2,1,0:T(8,128)(2,1)S(1)} %stage_tiles.2.refs_9_.refs_7_) | copy-start | bytes 25165828
  45.6 9.4 %collective-permute-start.11 = (bf16[32,4224]{1,0:T(8,128)(2,1)S(1)}, bf16[32,4224]{1,0:T(8,128)(2,1)S(1)}, u32[]{:S(2)}, u32[]{:S(2)}) collective-permute-start(bf16[32,4224]{1,0:T(8,128)(2,1)S(1)} %get-tuple-element.43), channel_id=1, source_target_pairs={{0,16},{8,24},{16,0},{24,8},{1,17},{9,25},{17,1},{25,9},{2,18},{10... | collective-permute-start | bytes 811016 | tf_op jit(solution)/shard_map/ppermute | solution.py:18
  47.1 12.7 %collective-permute-start.14 = (bf16[32,4224]{1,0:T(8,128)(2,1)S(1)}, bf16[32,4224]{1,0:T(8,128)(2,1)S(1)}, u32[]{:S(2)}, u32[]{:S(2)}) collective-permute-start(bf16[32,4224]{1,0:T(8,128)(2,1)S(1)} %get-tuple-element.46), channel_id=1, source_target_pairs={{0,24},{8,16},{16,8},{24,0},{1,25},{9,17},{17,9},{25,1},{2,26},{10... | collective-permute-start | bytes 811016 | tf_op jit(solution)/shard_map/ppermute | solution.py:18
  47.8 24.5 %collective-permute-start.12 = (bf16[32,2048]{1,0:T(8,128)(2,1)S(1)}, bf16[32,2048]{1,0:T(8,128)(2,1)S(1)}, u32[]{:S(2)}, u32[]{:S(2)}) collective-permute-start(bf16[32,2048]{1,0:T(8,128)(2,1)S(1)} %get-tuple-element.44), channel_id=1, source_target_pairs={{0,16},{8,24},{16,0},{24,8},{1,17},{9,25},{17,1},{25,9},{2,18},{10... | collective-permute-start | bytes 393224 | tf_op jit(solution)/shard_map/ppermute | solution.py:18
  49.3 23.0 %collective-permute-start.15 = (bf16[32,2048]{1,0:T(8,128)(2,1)S(1)}, bf16[32,2048]{1,0:T(8,128)(2,1)S(1)}, u32[]{:S(2)}, u32[]{:S(2)}) collective-permute-start(bf16[32,2048]{1,0:T(8,128)(2,1)S(1)} %get-tuple-element.47), channel_id=1, source_target_pairs={{0,24},{8,16},{16,8},{24,0},{1,25},{9,17},{17,9},{25,1},{2,26},{10... | collective-permute-start | bytes 393224 | tf_op jit(solution)/shard_map/ppermute | solution.py:18
  55.0 17.3 %collective-permute-start.13 = (bf16[32,2048]{1,0:T(8,128)(2,1)S(1)}, bf16[32,2048]{1,0:T(8,128)(2,1)S(1)}, u32[]{:S(2)}, u32[]{:S(2)}) collective-permute-start(bf16[32,2048]{1,0:T(8,128)(2,1)S(1)} %get-tuple-element.45), channel_id=1, source_target_pairs={{0,16},{8,24},{16,0},{24,8},{1,17},{9,25},{17,1},{25,9},{2,18},{10... | collective-permute-start | bytes 393224 | tf_op jit(solution)/shard_map/ppermute | solution.py:18
  59.8 12.5 %collective-permute-start.16 = (bf16[32,2048]{1,0:T(8,128)(2,1)S(1)}, bf16[32,2048]{1,0:T(8,128)(2,1)S(1)}, u32[]{:S(2)}, u32[]{:S(2)}) collective-permute-start(bf16[32,2048]{1,0:T(8,128)(2,1)S(1)} %get-tuple-element.48), channel_id=1, source_target_pairs={{0,24},{8,16},{16,8},{24,0},{1,25},{9,17},{17,9},{25,1},{2,26},{10... | collective-permute-start | bytes 393224 | tf_op jit(solution)/shard_map/ppermute | solution.py:18
  65.1 7.2 %slice-start = ((s8[8388608]{0:T(1024)(128)(4,1)}), s8[4194304]{0:T(1024)(128)(4,1)S(1)}, s32[]{:S(2)}) async-start(s8[8388608]{0:T(1024)(128)(4,1)} %bitcast.18), calls=%async_computation | async-start | bytes 8388608
  68.7 3.6 %slice-start.1 = ((s8[8388608]{0:T(1024)(128)(4,1)}), s8[4194304]{0:T(1024)(128)(4,1)S(1)}, s32[]{:S(2)}) async-start(s8[8388608]{0:T(1024)(128)(4,1)} %bitcast.18), calls=%async_computation.1 | async-start | bytes 8388608
  68.7 9.6 %copy-start.2 = (bf16[128,1024]{1,0:T(8,128)(2,1)S(1)}, bf16[128,1024]{1,0:T(8,128)(2,1)}, u32[]{:S(2)}) copy-start(bf16[128,1024]{1,0:T(8,128)(2,1)} %refs_11_.1) | copy-start | bytes 786436
  76.4 9.1 %collective-permute-start.17 = (bf16[32,1024]{1,0:T(8,128)(2,1)S(1)}, bf16[32,1024]{1,0:T(8,128)(2,1)S(1)}, u32[]{:S(2)}, u32[]{:S(2)}) collective-permute-start(bf16[32,1024]{1,0:T(8,128)(2,1)S(1)} %get-tuple-element.74), channel_id=1, source_target_pairs={{0,8},{8,0},{16,24},{24,16},{1,9},{9,1},{17,25},{25,17},{2,10},{10... | collective-permute-start | bytes 196616 | tf_op jit(solution)/shard_map/ppermute | solution.py:18
  76.5 9.0 %collective-permute-start.18 = (bf16[32,1024]{1,0:T(8,128)(2,1)S(1)}, bf16[32,1024]{1,0:T(8,128)(2,1)S(1)}, u32[]{:S(2)}, u32[]{:S(2)}) collective-permute-start(bf16[32,1024]{1,0:T(8,128)(2,1)S(1)} %get-tuple-element.73), channel_id=1, source_target_pairs={{0,16},{8,24},{16,0},{24,8},{1,17},{9,25},{17,1},{25,9},{2,18},{10... | collective-permute-start | bytes 196616 | tf_op jit(solution)/shard_map/ppermute | solution.py:18
  77.1 8.4 %collective-permute-start.19 = (bf16[32,1024]{1,0:T(8,128)(2,1)S(1)}, bf16[32,1024]{1,0:T(8,128)(2,1)S(1)}, u32[]{:S(2)}, u32[]{:S(2)}) collective-permute-start(bf16[32,1024]{1,0:T(8,128)(2,1)S(1)} %get-tuple-element.72), channel_id=1, source_target_pairs={{0,24},{8,16},{16,8},{24,0},{1,25},{9,17},{17,9},{25,1},{2,26},{10... | collective-permute-start | bytes 196616 | tf_op jit(solution)/shard_map/ppermute | solution.py:18
  86.0 15.1 %collective-permute-start.23 = (bf16[128,1024]{1,0:T(8,128)(2,1)S(1)}, bf16[128,1024]{1,0:T(8,128)(2,1)S(1)}, u32[]{:S(2)}, u32[]{:S(2)}) collective-permute-start(bf16[128,1024]{1,0:T(8,128)(2,1)S(1)} %get-tuple-element.49.refs_0_.refs_1_), channel_id=1, source_target_pairs={{0,4},{1,5},{2,6},{3,7},{4,0},{5,1},{6,2},{7,3},{8,12},{9,13},{10,... | collective-permute-start | bytes 786440 | tf_op jit(solution)/shard_map/ppermute | solution.py:18
  87.0 16.1 %collective-permute-start.21 = (bf16[128,1024]{1,0:T(8,128)(2,1)S(1)}, bf16[128,1024]{1,0:T(8,128)(2,1)S(1)}, u32[]{:S(2)}, u32[]{:S(2)}) collective-permute-start(bf16[128,1024]{1,0:T(8,128)(2,1)S(1)} %get-tuple-element.49.refs_0_.refs_1_), channel_id=1, source_target_pairs={{0,2},{1,3},{2,0},{3,1},{4,6},{5,7},{6,4},{7,5},{8,10},{9,11},{10,... | collective-permute-start | bytes 786440 | tf_op jit(solution)/shard_map/ppermute | solution.py:18
  101.1 9.2 %collective-permute-start.24 = (bf16[128,1024]{1,0:T(8,128)(2,1)S(1)}, bf16[128,1024]{1,0:T(8,128)(2,1)S(1)}, u32[]{:S(2)}, u32[]{:S(2)}) collective-permute-start(bf16[128,1024]{1,0:T(8,128)(2,1)S(1)} %collective-permute-done.23.refs_1_.refs_4_.refs_5_), channel_id=1, source_target_pairs={{0,1},{1,0},{2,3},{3,2},{4,5},{5,4},{6,7},{7,6},{8,9},{9,8},{10,11... | collective-permute-start | bytes 786440 | tf_op jit(solution)/shard_map/ppermute | solution.py:18
  101.6 14.2 %collective-permute-start.20 = (bf16[128,1024]{1,0:T(8,128)(2,1)S(1)}, bf16[128,1024]{1,0:T(8,128)(2,1)S(1)}, u32[]{:S(2)}, u32[]{:S(2)}) collective-permute-start(bf16[128,1024]{1,0:T(8,128)(2,1)S(1)} %get-tuple-element.49.refs_0_.refs_1_), channel_id=1, source_target_pairs={{0,1},{1,0},{2,3},{3,2},{4,5},{5,4},{6,7},{7,6},{8,9},{9,8},{10,11... | collective-permute-start | bytes 786440 | tf_op jit(solution)/shard_map/ppermute | solution.py:18
  103.1 17.4 %collective-permute-start.25 = (bf16[128,1024]{1,0:T(8,128)(2,1)S(1)}, bf16[128,1024]{1,0:T(8,128)(2,1)S(1)}, u32[]{:S(2)}, u32[]{:S(2)}) collective-permute-start(bf16[128,1024]{1,0:T(8,128)(2,1)S(1)} %collective-permute-done.23.refs_1_.refs_4_.refs_5_), channel_id=1, source_target_pairs={{0,2},{1,3},{2,0},{3,1},{4,6},{5,7},{6,4},{7,5},{8,10},{9,11},{10,... | collective-permute-start | bytes 786440 | tf_op jit(solution)/shard_map/ppermute | solution.py:18
  103.1 17.4 %collective-permute-start.22 = (bf16[128,1024]{1,0:T(8,128)(2,1)S(1)}, bf16[128,1024]{1,0:T(8,128)(2,1)S(1)}, u32[]{:S(2)}, u32[]{:S(2)}) collective-permute-start(bf16[128,1024]{1,0:T(8,128)(2,1)S(1)} %collective-permute-done.21.refs_0_.refs_2_.refs_3_), channel_id=1, source_target_pairs={{0,1},{1,0},{2,3},{3,2},{4,5},{5,4},{6,7},{7,6},{8,9},{9,8},{10,11... | collective-permute-start | bytes 786440 | tf_op jit(solution)/shard_map/ppermute | solution.py:18
  110.2 10.3 %collective-permute-start.26 = (bf16[128,1024]{1,0:T(8,128)(2,1)S(1)}, bf16[128,1024]{1,0:T(8,128)(2,1)S(1)}, u32[]{:S(2)}, u32[]{:S(2)}) collective-permute-start(bf16[128,1024]{1,0:T(8,128)(2,1)S(1)} %collective-permute-done.24.refs_0_.refs_5_.refs_6_.refs_1_), channel_id=1, source_target_pairs={{0,2},{1,3},{2,0},{3,1},{4,6},{5,7},{6,4},{7,5},{8,10},{9,11},{10,... | collective-permute-start | bytes 786440 | tf_op jit(solution)/shard_map/ppermute | solution.py:18
  120.9 25.9 %collective-permute-start.27 = (bf16[32,8320]{1,0:T(8,128)(2,1)S(1)}, bf16[32,8320]{1,0:T(8,128)(2,1)S(1)}, u32[]{:S(2)}, u32[]{:S(2)}) collective-permute-start(bf16[32,8320]{1,0:T(8,128)(2,1)S(1)} %pick_rows.12), channel_id=1, source_target_pairs={{0,8},{8,0},{16,24},{24,16},{1,9},{9,1},{17,25},{25,17},{2,10},{10... | collective-permute-start | bytes 1597448 | tf_op jit(solution)/shard_map/ppermute | solution.py:18
  121.3 9.4 %collective-permute-start.28 = (bf16[32,4224]{1,0:T(8,128)(2,1)S(1)}, bf16[32,4224]{1,0:T(8,128)(2,1)S(1)}, u32[]{:S(2)}, u32[]{:S(2)}) collective-permute-start(bf16[32,4224]{1,0:T(8,128)(2,1)S(1)} %get-tuple-element.59), channel_id=1, source_target_pairs={{0,16},{8,24},{16,0},{24,8},{1,17},{9,25},{17,1},{25,9},{2,18},{10... | collective-permute-start | bytes 811016 | tf_op jit(solution)/shard_map/ppermute | solution.py:18
  121.9 13.7 %collective-permute-start.31 = (bf16[32,4224]{1,0:T(8,128)(2,1)S(1)}, bf16[32,4224]{1,0:T(8,128)(2,1)S(1)}, u32[]{:S(2)}, u32[]{:S(2)}) collective-permute-start(bf16[32,4224]{1,0:T(8,128)(2,1)S(1)} %get-tuple-element.62), channel_id=1, source_target_pairs={{0,24},{8,16},{16,8},{24,0},{1,25},{9,17},{17,9},{25,1},{2,26},{10... | collective-permute-start | bytes 811016 | tf_op jit(solution)/shard_map/ppermute | solution.py:18
  126.9 19.3 %collective-permute-start.29 = (bf16[32,2048]{1,0:T(8,128)(2,1)S(1)}, bf16[32,2048]{1,0:T(8,128)(2,1)S(1)}, u32[]{:S(2)}, u32[]{:S(2)}) collective-permute-start(bf16[32,2048]{1,0:T(8,128)(2,1)S(1)} %get-tuple-element.60), channel_id=1, source_target_pairs={{0,16},{8,24},{16,0},{24,8},{1,17},{9,25},{17,1},{25,9},{2,18},{10... | collective-permute-start | bytes 393224 | tf_op jit(solution)/shard_map/ppermute | solution.py:18
  127.5 18.8 %collective-permute-start.32 = (bf16[32,2048]{1,0:T(8,128)(2,1)S(1)}, bf16[32,2048]{1,0:T(8,128)(2,1)S(1)}, u32[]{:S(2)}, u32[]{:S(2)}) collective-permute-start(bf16[32,2048]{1,0:T(8,128)(2,1)S(1)} %get-tuple-element.63), channel_id=1, source_target_pairs={{0,24},{8,16},{16,8},{24,0},{1,25},{9,17},{17,9},{25,1},{2,26},{10... | collective-permute-start | bytes 393224 | tf_op jit(solution)/shard_map/ppermute | solution.py:18
  130.7 15.5 %collective-permute-start.30 = (bf16[32,2048]{1,0:T(8,128)(2,1)S(1)}, bf16[32,2048]{1,0:T(8,128)(2,1)S(1)}, u32[]{:S(2)}, u32[]{:S(2)}) collective-permute-start(bf16[32,2048]{1,0:T(8,128)(2,1)S(1)} %get-tuple-element.61), channel_id=1, source_target_pairs={{0,16},{8,24},{16,0},{24,8},{1,17},{9,25},{17,1},{25,9},{2,18},{10... | collective-permute-start | bytes 393224 | tf_op jit(solution)/shard_map/ppermute | solution.py:18
  135.6 11.2 %collective-permute-start.33 = (bf16[32,2048]{1,0:T(8,128)(2,1)S(1)}, bf16[32,2048]{1,0:T(8,128)(2,1)S(1)}, u32[]{:S(2)}, u32[]{:S(2)}) collective-permute-start(bf16[32,2048]{1,0:T(8,128)(2,1)S(1)} %get-tuple-element.64), channel_id=1, source_target_pairs={{0,24},{8,16},{16,8},{24,0},{1,25},{9,17},{17,9},{25,1},{2,26},{10... | collective-permute-start | bytes 393224 | tf_op jit(solution)/shard_map/ppermute | solution.py:18
  150.9 9.1 %collective-permute-start.34 = (bf16[32,1024]{1,0:T(8,128)(2,1)S(1)}, bf16[32,1024]{1,0:T(8,128)(2,1)S(1)}, u32[]{:S(2)}, u32[]{:S(2)}) collective-permute-start(bf16[32,1024]{1,0:T(8,128)(2,1)S(1)} %get-tuple-element.71), channel_id=1, source_target_pairs={{0,8},{8,0},{16,24},{24,16},{1,9},{9,1},{17,25},{25,17},{2,10},{10... | collective-permute-start | bytes 196616 | tf_op jit(solution)/shard_map/ppermute | solution.py:18
  151.3 8.7 %collective-permute-start.35 = (bf16[32,1024]{1,0:T(8,128)(2,1)S(1)}, bf16[32,1024]{1,0:T(8,128)(2,1)S(1)}, u32[]{:S(2)}, u32[]{:S(2)}) collective-permute-start(bf16[32,1024]{1,0:T(8,128)(2,1)S(1)} %get-tuple-element.70), channel_id=1, source_target_pairs={{0,16},{8,24},{16,0},{24,8},{1,17},{9,25},{17,1},{25,9},{2,18},{10... | collective-permute-start | bytes 196616 | tf_op jit(solution)/shard_map/ppermute | solution.py:18
  152.1 7.9 %collective-permute-start.36 = (bf16[32,1024]{1,0:T(8,128)(2,1)S(1)}, bf16[32,1024]{1,0:T(8,128)(2,1)S(1)}, u32[]{:S(2)}, u32[]{:S(2)}) collective-permute-start(bf16[32,1024]{1,0:T(8,128)(2,1)S(1)} %get-tuple-element.69), channel_id=1, source_target_pairs={{0,24},{8,16},{16,8},{24,0},{1,25},{9,17},{17,9},{25,1},{2,26},{10... | collective-permute-start | bytes 196616 | tf_op jit(solution)/shard_map/ppermute | solution.py:18
